TPU v7x, 512 devices: a whole 4x4x16 slice. The times are simulated.
512 devices in a mesh: kx: 16 (over z_hi, x), ky: 32 (over y, z_lo, core).
Axes of the slice: x: 4, y: 4, z: 16 (z_hi: 4, z_lo: 4; z = z_hi * 4 + z_lo), core: 2. Of those that a mesh axis runs over, the one named last changes fastest.
Arguments:
- states: bfloat16 [512, 4096, 128], P(('kx', 'ky')), may hold values from -6 to 6
- energies: bfloat16 [512, 128], P(('kx', 'ky')), may hold values from -2 to 2
- external: float32 [1, 4096], replicated, may hold values from -6 to 6
- reorder: int32 [2, 512, 4096], P(None, ('kx', 'ky')), may hold values from 0 to 4095, each once within a row
Outputs:
- band_response: float32 [512, 2, 1, 128, 128], P(('kx', 'ky'))
- density: float32 [2, 1, 4096], replicated
Inputs may be any that keep to these rules, and one draw needn't show every extreme that they name: Each row reorder[q, k] is a permutation of the 4096 grid components.
All inputs are finite; a program needn't handle non-finite values.
Results may differ from a plain program's by a relative error of at most 0.0029.
Values may be sent and summed in bfloat16 or wider, within the bound.
No kernel may reach another device: no remote copies, remote signals or barrier semaphores. Data moves between devices by JAX's collectives and lax.ppermute only.
A program may use at most 64 MiB of HBM per device.

v0:
```python
import math

import jax
import jax.numpy as jnp
from jax import lax
from jax.sharding import PartitionSpec as P

GX = 64
GY = 64
NQ = 2
ITERS = 2


SMEAR = 0.5
FERMI = 0.0
SCREEN = 4.0


def passed_along(value, axis, steps):
    count = lax.axis_size(axis)
    pairs = [(source, (source + steps) % count) for source in range(count)]
    return lax.ppermute(value, axis, pairs)


def hartley_table(length):
    positions = jnp.arange(length, dtype=jnp.int32)
    phases = positions[:, None] * positions[None, :] % length
    angles = phases.astype(jnp.float32) * (2.0 * math.pi / length)
    return (jnp.cos(angles) + jnp.sin(angles)) / math.sqrt(length)


def screening(len_x, len_y):
    freq_x = jnp.arange(len_x, dtype=jnp.int32)
    freq_x = jnp.minimum(freq_x, len_x - freq_x).astype(jnp.float32)
    freq_y = jnp.arange(len_y, dtype=jnp.int32)
    freq_y = jnp.minimum(freq_y, len_y - freq_y).astype(jnp.float32)
    return 1.0 / (1.0 + (freq_x[:, None] ** 2 + freq_y[None, :] ** 2) / SCREEN)


def coulomb(density):
    fields = density.reshape(density.shape[:-1] + (GX, GY))
    table_x = hartley_table(GX)
    table_y = hartley_table(GY)
    spectra = jnp.einsum(
        "pi,abij,jq->abpq", table_x, fields, table_y, precision=lax.Precision.HIGHEST
    )
    spectra = spectra * screening(GX, GY)
    result = jnp.einsum(
        "pi,abij,jq->abpq", table_x, spectra, table_y, precision=lax.Precision.HIGHEST
    )
    return result.reshape(density.shape)


def occupation(energy):
    return 1.0 / (1.0 + jnp.exp((energy - FERMI) / SMEAR))


def respond(orbital, energy, far_states, far_energy, potential):
    energy = energy.astype(jnp.float32)
    far_energy = far_energy.astype(jnp.float32)
    weighted = (potential[:, :, None] * orbital[None].astype(jnp.float32)).astype(jnp.bfloat16)
    band_mats = jnp.einsum("gm,agn->amn", far_states, weighted, preferred_element_type=jnp.float32)
    band_mats = band_mats * (1.0 / math.sqrt(orbital.shape[0]))
    gap_matrix = far_energy[:, None] - energy[None, :]
    weight = (
        (occupation(energy)[None, :] - occupation(far_energy)[:, None])
        * gap_matrix
        / (gap_matrix * gap_matrix + SMEAR * SMEAR)
    )
    response = weight[None] * band_mats
    response_low = response.astype(jnp.bfloat16)
    orbitals_out = jnp.einsum(
        "gm,amn->agn", far_states, response_low, preferred_element_type=jnp.float32
    )
    orbitals_out = orbitals_out * (1.0 / math.sqrt(orbital.shape[1]))
    contrib = jnp.sum(orbital[None].astype(jnp.float32) * orbitals_out, axis=2)
    return (response, contrib)


def partner_of(q_index, orbital, energy, reorder):
    if q_index == 0:
        far_states, far_energy = passed_along((orbital, energy), "kx", -1)
    else:
        far_states, far_energy = passed_along((orbital, energy), "ky", -1)
    return (jnp.take(far_states, reorder[q_index, 0], axis=0), far_energy)


def shards(states, energies, external, reorder):
    orbital = states[0]
    energy = energies[0]
    kpoint_count = lax.axis_size("kx") * lax.axis_size("ky")
    grid_size = orbital.shape[0]
    potential = jnp.broadcast_to(external[None], (NQ, external.shape[0], grid_size))
    fetched_all = [None for q_index in range(NQ)]
    fetched_all = [partner_of(q_index, orbital, energy, reorder) for q_index in range(NQ)]
    for rounds in range(ITERS):
        responses = []
        density_parts = []
        for q_index in range(NQ):
            far_states, far_energy = fetched_all[q_index]
            response, contrib = respond(orbital, energy, far_states, far_energy, potential[q_index])
            responses.append(response)
            contrib = lax.psum(contrib, ("kx", "ky"))
            density_parts.append(contrib)
        density = jnp.stack(density_parts)
        density = density * (1.0 / math.sqrt(kpoint_count))
        if rounds + 1 < ITERS:
            potential = external[None] + coulomb(density)
    return (jnp.stack(responses)[None], density)


def solution(mesh):
    return jax.shard_map(
        shards,
        mesh=mesh,
        in_specs=(
            P(("kx", "ky"), None, None),
            P(("kx", "ky"), None),
            P(),
            P(None, ("kx", "ky"), None),
        ),
        out_specs=(P(("kx", "ky"), None, None, None, None), P()),
        check_vma=False,
    )
```

profile of v0, /device:TPU:1, one launch (start us, length us, event | category | flops | bytes accessed | tf_op | source)
XLA Modules:
  0.0 359.3 jit_solution(14189310008102383190)
XLA Ops:
  0.6 15.5 %collective-permute-start.1 = (bf16[4096,128]{1,0:T(8,128)(2,1)}, bf16[4096,128]{1,0:T(8,128)(2,1)S(1)}, u32[]{:S(2)}, u32[]{:S(2)}) collective-permute-start(bf16[4096,128]{1,0:T(8,128)(2,1)} %bitcast.125), channel_id=1, source_target_pairs={{0,480},{32,0},{64,32},{96,64},{128,96},{160,128},{192,160},{224,1... | collective-permute-start | bytes 3145736 | tf_op jit(solution)/shard_map/ppermute | solution.py:22
  16.1 2.9 collective-permute-start.3
  19.0 2.5 collective-permute-start
  21.4 5.7 %collective-permute-start.2 = (bf16[128]{0:T(256)(128)(2,1)}, bf16[128]{0:T(256)(128)(2,1)S(1)}, u32[]{:S(2)}, u32[]{:S(2)}) collective-permute-start(bf16[128]{0:T(256)(128)(2,1)} %bitcast.141), channel_id=1, source_target_pairs={{0,31},{1,0},{2,1},{3,2},{4,3},{5,4},{6,5},{7,6},{8,7},{9,8},{10,9... | collective-permute-start | bytes 776 | tf_op jit(solution)/shard_map/ppermute | solution.py:22
  27.2 0.7 fusion.105
  28.1 0.7 convert_bitcast_fusion
  28.7 0.7 divide_bitcast_fusion
  29.4 2.3 copy.6
  31.7 74.8 %collective-permute-done = bf16[128]{0:T(256)(128)(2,1)S(1)} collective-permute-done((bf16[128]{0:T(256)(128)(2,1)}, bf16[128]{0:T(256)(128)(2,1)S(1)}, u32[]{:S(2)}, u32[]{:S(2)}) %collective-permute-start) | collective-permute-done | bytes 288 | tf_op jit(solution)/shard_map/ppermute | solution.py:22
  106.5 11.6 %collective-permute-done.2 = bf16[128]{0:T(256)(128)(2,1)S(1)} collective-permute-done((bf16[128]{0:T(256)(128)(2,1)}, bf16[128]{0:T(256)(128)(2,1)S(1)}, u32[]{:S(2)}, u32[]{:S(2)}) %collective-permute-start.2) | collective-permute-done | bytes 288 | tf_op jit(solution)/shard_map/ppermute | solution.py:22
  118.1 12.1 %gather_fusion = bf16[4096,128]{1,0:T(8,128)(2,1)S(1)} fusion(bf16[4096,128]{1,0:T(8,128)(2,1)S(1)} %collective-permute-done.1, s32[4096]{0:T(1024)S(1)} %fusion.74), kind=kCustom, calls=%fused_computation.clone | custom fusion | bytes 2113536 | tf_op jit(solution)/shard_map/jit(_take)/gather | solution.py:85
  130.3 3.1 fusion.7
  133.4 12.1 %gather_fusion.1 = bf16[4096,128]{1,0:T(8,128)(2,1)S(1)} fusion(bf16[4096,128]{1,0:T(8,128)(2,1)S(1)} %collective-permute-done.3, s32[4096]{0:T(1024)S(1)} %fusion.75), kind=kCustom, calls=%fused_computation.1.clone | custom fusion | bytes 2113536 | tf_op jit(solution)/shard_map/jit(_take)/gather | solution.py:85
  145.6 3.1 fusion.8
  148.7 104.2 %all-reduce.1 = (f32[1,64,64]{2,1,0:T(8,128)S(1)}, f32[1,64,64]{2,1,0:T(8,128)S(1)}) all-reduce(f32[1,64,64]{2,1,0:T(8,128)S(1)} %stack.28, f32[1,64,64]{2,1,0:T(8,128)S(1)} %stack.27), channel_id=1, replica_groups=mesh['kx'=16,'ky'=32] {'kx','ky'}, use_global_device_ids=true, to_apply=%region_3.5 | all-reduce | flops 8192 | bytes 65536 | tf_op jit(solution)/shard_map/psum | solution.py:103
  252.9 0.4 fusion.40
  253.3 0.3 convolution_multiply_fusion.6
  254.5 0.8 fusion.14
  255.4 1.1 fusion.9
  256.4 0.8 fusion.12
  257.2 1.1 fusion.10
  258.3 0.8 copy.7
  259.1 99.5 %all-reduce = (f32[1,1,4096]{2,1,0:T(1,128)S(1)}, f32[1,1,4096]{2,1,0:T(1,128)S(1)}) all-reduce(f32[1,1,4096]{2,1,0:T(1,128)S(1)} %bitcast.137, f32[1,1,4096]{2,1,0:T(1,128)S(1)} %bitcast.136), channel_id=1, replica_groups=mesh['kx'=16,'ky'=32] {'kx','ky'}, use_global_device_ids=true, to_apply=%region_7.9 | all-reduce | flops 8192 | bytes 65536 | tf_op jit(solution)/shard_map/psum | solution.py:103
  358.6 0.7 maximum_multiply_fusion.2
  (24 shorter events, 1.1 us)
Async XLA Ops:
  0.6 117.5 %collective-permute-start.1 = (bf16[4096,128]{1,0:T(8,128)(2,1)}, bf16[4096,128]{1,0:T(8,128)(2,1)S(1)}, u32[]{:S(2)}, u32[]{:S(2)}) collective-permute-start(bf16[4096,128]{1,0:T(8,128)(2,1)} %bitcast.125), channel_id=1, source_target_pairs={{0,480},{32,0},{64,32},{96,64},{128,96},{160,128},{192,160},{224,1... | collective-permute-start | bytes 3145736 | tf_op jit(solution)/shard_map/ppermute | solution.py:22
  16.1 117.3 %collective-permute-start.3 = (bf16[4096,128]{1,0:T(8,128)(2,1)}, bf16[4096,128]{1,0:T(8,128)(2,1)S(1)}, u32[]{:S(2)}, u32[]{:S(2)}) collective-permute-start(bf16[4096,128]{1,0:T(8,128)(2,1)} %bitcast.126), channel_id=1, source_target_pairs={{0,31},{1,0},{2,1},{3,2},{4,3},{5,4},{6,5},{7,6},{8,7},{9,8},{10,9... | collective-permute-start | bytes 3145736 | tf_op jit(solution)/shard_map/ppermute | solution.py:22
  19.0 87.5 %collective-permute-start = (bf16[128]{0:T(256)(128)(2,1)}, bf16[128]{0:T(256)(128)(2,1)S(1)}, u32[]{:S(2)}, u32[]{:S(2)}) collective-permute-start(bf16[128]{0:T(256)(128)(2,1)} %bitcast.140), channel_id=1, source_target_pairs={{0,480},{32,0},{64,32},{96,64},{128,96},{160,128},{192,160},{224,1... | collective-permute-start | bytes 776 | tf_op jit(solution)/shard_map/ppermute | solution.py:22
  21.4 96.6 %collective-permute-start.2 = (bf16[128]{0:T(256)(128)(2,1)}, bf16[128]{0:T(256)(128)(2,1)S(1)}, u32[]{:S(2)}, u32[]{:S(2)}) collective-permute-start(bf16[128]{0:T(256)(128)(2,1)} %bitcast.141), channel_id=1, source_target_pairs={{0,31},{1,0},{2,1},{3,2},{4,3},{5,4},{6,5},{7,6},{8,7},{9,8},{10,9... | collective-permute-start | bytes 776 | tf_op jit(solution)/shard_map/ppermute | solution.py:22
  118.1 12.2 %copy-start.1 = (f32[1,4096]{1,0:T(1,128)S(1)}, f32[1,4096]{1,0:T(1,128)}, u32[]{:S(2)}) copy-start(f32[1,4096]{1,0:T(1,128)} %param.8) | copy-start | bytes 49156
  148.7 105.9 %copy-start = (bf16[1,4096,128]{1,2,0:T(8,128)(2,1)S(1)}, bf16[1,4096,128]{1,2,0:T(8,128)(2,1)}, u32[]{:S(2)}) copy-start(bf16[1,4096,128]{1,2,0:T(8,128)(2,1)} %copy.6) | copy-start | bytes 3145732
where the time goes:
time: 360 us; the launch traced here: 359 us
  blocking collectives  204 us (57%)
  waiting for transfers between devices  86.4 us (24%)
  local copies, waits for them, and re-layouts  28.3 us (8%)
  starting transfers between devices  26.5 us (7%)
  matrix products  11.3 us (3%)
    psum x2, blocking collectives, shards(): contrib = lax.psum(contrib, ('kx', 'ky'))  204 us
    ppermute x4, waiting for transfers between devices, passed_along(): return lax.ppermute(value, axis, pairs)  86.4 us
    ppermute x4, starting transfers between devices, passed_along(): return lax.ppermute(value, axis, pairs)  26.5 us
    gather x2, local copies, waits for them, and re-layouts, partner_of(): return (jnp.take(far_states, reorder[q_index, 0], axis=0), far_energy)  24.3 us
    dot_general x4, matrix products, respond(): jnp.einsum('gm,amn->agn', far_states, response_low, preferred_element_typ...  8.27 us
  transfers between devices with their start and end apart: 4, of which 2 were waited for; matrix products, arithmetic and copies ran while one was open for 5% of the time, Pallas kernels for 0%

commit v1 on v0

--- a/solution.py
+++ b/solution.py
@@ -3,7 +3,14 @@
 import jax
 import jax.numpy as jnp
 from jax import lax
-from jax.sharding import PartitionSpec as P
+from jax.sharding import Mesh, PartitionSpec as P
+
+AXES = ("zh", "x", "y", "zl", "core")
+AXIS_SIZES = (4, 4, 4, 4, 2)
+KX = ("zh", "x")
+KY = ("y", "zl", "core")
+PLANE = ("x", "y", "core")
+COLUMN = ("zh", "zl")
 
 GX = 64
 GY = 64
@@ -20,6 +27,21 @@
     count = lax.axis_size(axis)
     pairs = [(source, (source + steps) % count) for source in range(count)]
     return lax.ppermute(value, axis, pairs)
+
+
+def exchange(value, axes):
+    return lax.all_to_all(value, axes, 0, 0, tiled=True)
+
+
+def summed_everywhere(value):
+    plane = lax.axis_size(PLANE)
+    column = lax.axis_size(COLUMN)
+    chunks = value.reshape(plane, -1, 128)
+    part = jnp.sum(exchange(chunks, PLANE), axis=0)
+    copies = jnp.broadcast_to(part[None], (column,) + part.shape)
+    part = jnp.sum(exchange(copies, COLUMN), axis=0)
+    copies = jnp.broadcast_to(part[None], (plane,) + part.shape)
+    return exchange(copies, PLANE).reshape(value.shape)
 
 
 def hartley_table(length):
@@ -79,19 +101,18 @@
 
 def partner_of(q_index, orbital, energy, reorder):
     if q_index == 0:
-        far_states, far_energy = passed_along((orbital, energy), "kx", -1)
+        far_states, far_energy = passed_along((orbital, energy), KX, -1)
     else:
-        far_states, far_energy = passed_along((orbital, energy), "ky", -1)
+        far_states, far_energy = passed_along((orbital, energy), KY, -1)
     return (jnp.take(far_states, reorder[q_index, 0], axis=0), far_energy)
 
 
 def shards(states, energies, external, reorder):
     orbital = states[0]
     energy = energies[0]
-    kpoint_count = lax.axis_size("kx") * lax.axis_size("ky")
+    kpoint_count = lax.axis_size(AXES)
     grid_size = orbital.shape[0]
     potential = jnp.broadcast_to(external[None], (NQ, external.shape[0], grid_size))
-    fetched_all = [None for q_index in range(NQ)]
     fetched_all = [partner_of(q_index, orbital, energy, reorder) for q_index in range(NQ)]
     for rounds in range(ITERS):
         responses = []
@@ -100,9 +121,8 @@
             far_states, far_energy = fetched_all[q_index]
             response, contrib = respond(orbital, energy, far_states, far_energy, potential[q_index])
             responses.append(response)
-            contrib = lax.psum(contrib, ("kx", "ky"))
             density_parts.append(contrib)
-        density = jnp.stack(density_parts)
+        density = summed_everywhere(jnp.stack(density_parts))
         density = density * (1.0 / math.sqrt(kpoint_count))
         if rounds + 1 < ITERS:
             potential = external[None] + coulomb(density)
@@ -110,15 +130,16 @@
 
 
 def solution(mesh):
+    fine = Mesh(mesh.devices.reshape(AXIS_SIZES), AXES)
     return jax.shard_map(
         shards,
-        mesh=mesh,
+        mesh=fine,
         in_specs=(
-            P(("kx", "ky"), None, None),
-            P(("kx", "ky"), None),
+            P(AXES, None, None),
+            P(AXES, None),
             P(),
-            P(None, ("kx", "ky"), None),
+            P(None, AXES, None),
         ),
-        out_specs=(P(("kx", "ky"), None, None, None, None), P()),
+        out_specs=(P(AXES, None, None, None, None), P()),
         check_vma=False,
     )

time: 360 us -> 243 us (0.68)
  blocking collectives: 204 us -> 36.5 us
  waiting for transfers between devices: 86.4 us -> 112 us
  starting transfers between devices: 26.5 us -> 49.5 us
    psum x2 -> x0, blocking collectives: 204 us -> none  [shards(): contrib = lax.psum(contrib, ('kx', 'ky'))]
    all_to_all x0 -> x3, blocking collectives: none -> 36.5 us  [exchange(): return lax.all_to_all(value, axes, 0, 0, tiled=True)]
    all_to_all x0 -> x3, waiting for transfers between devices: none -> 25.3 us  [exchange(): return lax.all_to_all(value, axes, 0, 0, tiled=True)]
    all_to_all x0 -> x3, starting transfers between devices: none -> 23 us  [exchange(): return lax.all_to_all(value, axes, 0, 0, tiled=True)]
  transfers between devices with their start and end apart: 4 -> 7, of which waited for: 2 -> 5; matrix products, arithmetic and copies ran while one was open for 5% -> 8% of each run, Pallas kernels for 0% -> 0%
where the time goes in v1:
time: 243 us
  waiting for transfers between devices  112 us (46%)
  starting transfers between devices  49.5 us (20%)
  blocking collectives  36.5 us (15%)
  local copies, waits for them, and re-layouts  30.2 us (12%)
  matrix products  11.3 us (5%)
    ppermute x4, waiting for transfers between devices, passed_along(): return lax.ppermute(value, axis, pairs)  86.5 us
    all_to_all x3, blocking collectives, exchange(): return lax.all_to_all(value, axes, 0, 0, tiled=True)  36.5 us
    ppermute x4, starting transfers between devices, passed_along(): return lax.ppermute(value, axis, pairs)  26.5 us
    all_to_all x3, waiting for transfers between devices, exchange(): return lax.all_to_all(value, axes, 0, 0, tiled=True)  25.3 us
    gather x2, local copies, waits for them, and re-layouts, partner_of(): return (jnp.take(far_states, reorder[q_index, 0], axis=0), far_energy)  24.3 us
    all_to_all x3, starting transfers between devices, exchange(): return lax.all_to_all(value, axes, 0, 0, tiled=True)  23 us
    dot_general x4, matrix products, respond(): jnp.einsum('gm,amn->agn', far_states, response_low, preferred_element_typ...  8.27 us
  transfers between devices with their start and end apart: 7, of which 5 were waited for; matrix products, arithmetic and copies ran while one was open for 8% of the time, Pallas kernels for 0%

profile of v1, /device:TPU:1, one launch (start us, length us, event | category | flops | bytes accessed | tf_op | source)
XLA Modules:
  0.0 242.6 jit_solution(17479184853421071909)
XLA Ops:
  0.6 15.5 %collective-permute-start.1 = (bf16[4096,128]{1,0:T(8,128)(2,1)}, bf16[4096,128]{1,0:T(8,128)(2,1)S(1)}, u32[]{:S(2)}, u32[]{:S(2)}) collective-permute-start(bf16[4096,128]{1,0:T(8,128)(2,1)} %bitcast.133), channel_id=1, source_target_pairs={{0,480},{32,0},{64,32},{96,64},{128,96},{160,128},{192,160},{224,1... | collective-permute-start | bytes 3145736 | tf_op jit(solution)/shard_map/ppermute | solution.py:29
  16.1 2.9 %collective-permute-start.3 = (bf16[4096,128]{1,0:T(8,128)(2,1)}, bf16[4096,128]{1,0:T(8,128)(2,1)S(1)}, u32[]{:S(2)}, u32[]{:S(2)}) collective-permute-start(bf16[4096,128]{1,0:T(8,128)(2,1)} %bitcast.134), channel_id=1, source_target_pairs={{0,31},{1,0},{2,1},{3,2},{4,3},{5,4},{6,5},{7,6},{8,7},{9,8},{10,9... | collective-permute-start | bytes 3145736 | tf_op jit(solution)/shard_map/ppermute | solution.py:29
  19.0 2.5 %collective-permute-start = (bf16[128]{0:T(256)(128)(2,1)}, bf16[128]{0:T(256)(128)(2,1)S(1)}, u32[]{:S(2)}, u32[]{:S(2)}) collective-permute-start(bf16[128]{0:T(256)(128)(2,1)} %bitcast.151), channel_id=1, source_target_pairs={{0,480},{32,0},{64,32},{96,64},{128,96},{160,128},{192,160},{224,1... | collective-permute-start | bytes 776 | tf_op jit(solution)/shard_map/ppermute | solution.py:29
  21.4 5.7 %collective-permute-start.2 = (bf16[128]{0:T(256)(128)(2,1)}, bf16[128]{0:T(256)(128)(2,1)S(1)}, u32[]{:S(2)}, u32[]{:S(2)}) collective-permute-start(bf16[128]{0:T(256)(128)(2,1)} %bitcast.152), channel_id=1, source_target_pairs={{0,31},{1,0},{2,1},{3,2},{4,3},{5,4},{6,5},{7,6},{8,7},{9,8},{10,9... | collective-permute-start | bytes 776 | tf_op jit(solution)/shard_map/ppermute | solution.py:29
  29.3 2.3 copy.25
  31.6 74.9 %collective-permute-done = bf16[128]{0:T(256)(128)(2,1)S(1)} collective-permute-done((bf16[128]{0:T(256)(128)(2,1)}, bf16[128]{0:T(256)(128)(2,1)S(1)}, u32[]{:S(2)}, u32[]{:S(2)}) %collective-permute-start) | collective-permute-done | bytes 288 | tf_op jit(solution)/shard_map/ppermute | solution.py:29
  106.5 11.6 %collective-permute-done.2 = bf16[128]{0:T(256)(128)(2,1)S(1)} collective-permute-done((bf16[128]{0:T(256)(128)(2,1)}, bf16[128]{0:T(256)(128)(2,1)S(1)}, u32[]{:S(2)}, u32[]{:S(2)}) %collective-permute-start.2) | collective-permute-done | bytes 288 | tf_op jit(solution)/shard_map/ppermute | solution.py:29
  118.1 12.1 %gather_fusion = bf16[4096,128]{1,0:T(8,128)(2,1)S(1)} fusion(bf16[4096,128]{1,0:T(8,128)(2,1)S(1)} %collective-permute-done.1, s32[4096]{0:T(1024)S(1)} %fusion.71), kind=kCustom, calls=%fused_computation.clone | custom fusion | bytes 2113536 | tf_op jit(solution)/shard_map/jit(_take)/gather | solution.py:107
  130.3 3.1 %fusion.7 = f32[4096]{0:T(1024)S(1)} fusion(bf16[1,4096,128]{1,2,0:T(8,128)(2,1)} %copy.25, f32[4096]{0:T(1024)S(1)} %bitcast.142, f32[128]{0:T(128)S(1)} %convert_bitcast_fusion, f32[128]{0:T(128)S(1)} %convert_element_type.71, f32[128]{0:T(128)S(1)} %add_divide_fusion.2, f32[128]{0:T(128)S(1)} %divide_bitcast_fusion, ...), kind=kOutput, calls=%fused_computation.20 | convolution fusion | flops 273297408 | bytes 2136064 | tf_op jit(solution)/shard_map/gm,amn->agn/dot_general | solution.py:94
  133.4 12.1 %gather_fusion.1 = bf16[4096,128]{1,0:T(8,128)(2,1)S(1)} fusion(bf16[4096,128]{1,0:T(8,128)(2,1)S(1)} %collective-permute-done.3, s32[4096]{0:T(1024)S(1)} %fusion.72), kind=kCustom, calls=%fused_computation.1.clone | custom fusion | bytes 2113536 | tf_op jit(solution)/shard_map/jit(_take)/gather | solution.py:107
  145.5 3.1 %fusion.8 = f32[4096]{0:T(1024)S(1)} fusion(bf16[1,4096,128]{1,2,0:T(8,128)(2,1)} %copy.25, f32[4096]{0:T(1024)S(1)} %bitcast.143, f32[128]{0:T(128)S(1)} %convert_element_type.75, f32[128]{0:T(128)S(1)} %add_divide_fusion.1, f32[128]{0:T(128)S(1)} %convert_bitcast_fusion, f32[128]{0:T(128)S(1)} %divide_bitcast_fusion, ...), kind=kOutput, calls=%fused_computation.21 | convolution fusion | flops 273297408 | bytes 2136064 | tf_op jit(solution)/shard_map/gm,amn->agn/dot_general | solution.py:94
  148.7 11.9 %all_to_all.30 = f32[32,2,128]{2,1,0:T(2,128)S(1)} all-to-all(f32[32,2,128]{2,1,0:T(2,128)S(1)} %reshape.423), channel_id=1, replica_groups=mesh['zh'=4,'x'=4,'y'=4,'zl'=4,'core'=2] {'x','y','core'}, dimensions={0} | all-to-all | bytes 65536 | tf_op jit(solution)/shard_map/all_to_all | solution.py:33
  161.3 12.6 %all-to-all-start.1 = ((f32[16,2,128]{2,1,0:T(2,128)}), f32[16,2,128]{2,1,0:T(2,128)S(1)}, u32[]{:S(2)}, u32[]{:S(2)}) async-start(f32[16,2,128]{2,1,0:T(2,128)} %broadcast_in_dim.19), calls=%async_computation.1 | async-start | bytes 32768 | tf_op jit(solution)/shard_map/all_to_all | solution.py:33
  173.9 11.4 %all-to-all-done.1 = f32[16,2,128]{2,1,0:T(2,128)S(1)} async-done(((f32[16,2,128]{2,1,0:T(2,128)}), f32[16,2,128]{2,1,0:T(2,128)S(1)}, u32[]{:S(2)}, u32[]{:S(2)}) %all-to-all-start.1) | async-done | bytes 16416 | tf_op jit(solution)/shard_map/all_to_all | solution.py:33
  185.9 5.3 %all-to-all-start.2 = ((f32[32,2,128]{2,1,0:T(2,128)}), f32[32,2,128]{2,1,0:T(2,128)S(1)}, u32[]{:S(2)}, u32[]{:S(2)}) async-start(f32[32,2,128]{2,1,0:T(2,128)} %broadcast_in_dim.20), calls=%async_computation.2 | async-start | bytes 65536 | tf_op jit(solution)/shard_map/all_to_all | solution.py:33
  191.3 7.3 %all-to-all-done.2 = f32[32,2,128]{2,1,0:T(2,128)S(1)} async-done(((f32[32,2,128]{2,1,0:T(2,128)}), f32[32,2,128]{2,1,0:T(2,128)S(1)}, u32[]{:S(2)}, u32[]{:S(2)}) %all-to-all-start.2) | async-done | bytes 32800 | tf_op jit(solution)/shard_map/all_to_all | solution.py:33
  200.3 0.8 fusion.14
  201.1 1.1 fusion.9
  202.2 0.8 fusion.12
  203.0 1.1 fusion.10
  204.2 10.7 %all_to_all.31 = f32[32,2,128]{2,1,0:T(2,128)S(1)} all-to-all(f32[32,2,128]{2,1,0:T(2,128)S(1)} %reshape.429), channel_id=1, replica_groups=mesh['zh'=4,'x'=4,'y'=4,'zl'=4,'core'=2] {'x','y','core'}, dimensions={0} | all-to-all | bytes 65536 | tf_op jit(solution)/shard_map/all_to_all | solution.py:33
  215.0 13.9 %all_to_all.32 = f32[16,2,128]{2,1,0:T(2,128)S(1)} all-to-all(f32[16,2,128]{2,1,0:T(2,128)S(1)} %broadcast_in_dim.22), channel_id=1, replica_groups=mesh['zh'=4,'x'=4,'y'=4,'zl'=4,'core'=2] {'zh','zl'}, dimensions={0} | all-to-all | bytes 32768 | tf_op jit(solution)/shard_map/all_to_all | solution.py:33
  229.5 5.1 %all-to-all-start.5 = ((f32[32,2,128]{2,1,0:T(2,128)}), f32[32,2,128]{2,1,0:T(2,128)S(1)}, u32[]{:S(2)}, u32[]{:S(2)}) async-start(f32[32,2,128]{2,1,0:T(2,128)} %broadcast_in_dim.23), calls=%async_computation.5 | async-start | bytes 65536 | tf_op jit(solution)/shard_map/all_to_all | solution.py:33
  235.4 6.6 %all-to-all-done.5 = f32[32,2,128]{2,1,0:T(2,128)S(1)} async-done(((f32[32,2,128]{2,1,0:T(2,128)}), f32[32,2,128]{2,1,0:T(2,128)S(1)}, u32[]{:S(2)}, u32[]{:S(2)}) %all-to-all-start.5) | async-done | bytes 32800 | tf_op jit(solution)/shard_map/all_to_all | solution.py:33
  (43 shorter events, 7.4 us)
Async XLA Ops:
  0.6 117.5 %collective-permute-start.1 = (bf16[4096,128]{1,0:T(8,128)(2,1)}, bf16[4096,128]{1,0:T(8,128)(2,1)S(1)}, u32[]{:S(2)}, u32[]{:S(2)}) collective-permute-start(bf16[4096,128]{1,0:T(8,128)(2,1)} %bitcast.133), channel_id=1, source_target_pairs={{0,480},{32,0},{64,32},{96,64},{128,96},{160,128},{192,160},{224,1... | collective-permute-start | bytes 3145736 | tf_op jit(solution)/shard_map/ppermute | solution.py:29
  16.1 117.3 %collective-permute-start.3 = (bf16[4096,128]{1,0:T(8,128)(2,1)}, bf16[4096,128]{1,0:T(8,128)(2,1)S(1)}, u32[]{:S(2)}, u32[]{:S(2)}) collective-permute-start(bf16[4096,128]{1,0:T(8,128)(2,1)} %bitcast.134), channel_id=1, source_target_pairs={{0,31},{1,0},{2,1},{3,2},{4,3},{5,4},{6,5},{7,6},{8,7},{9,8},{10,9... | collective-permute-start | bytes 3145736 | tf_op jit(solution)/shard_map/ppermute | solution.py:29
  19.0 87.5 %collective-permute-start = (bf16[128]{0:T(256)(128)(2,1)}, bf16[128]{0:T(256)(128)(2,1)S(1)}, u32[]{:S(2)}, u32[]{:S(2)}) collective-permute-start(bf16[128]{0:T(256)(128)(2,1)} %bitcast.151), channel_id=1, source_target_pairs={{0,480},{32,0},{64,32},{96,64},{128,96},{160,128},{192,160},{224,1... | collective-permute-start | bytes 776 | tf_op jit(solution)/shard_map/ppermute | solution.py:29
  21.4 96.6 %collective-permute-start.2 = (bf16[128]{0:T(256)(128)(2,1)}, bf16[128]{0:T(256)(128)(2,1)S(1)}, u32[]{:S(2)}, u32[]{:S(2)}) collective-permute-start(bf16[128]{0:T(256)(128)(2,1)} %bitcast.152), channel_id=1, source_target_pairs={{0,31},{1,0},{2,1},{3,2},{4,3},{5,4},{6,5},{7,6},{8,7},{9,8},{10,9... | collective-permute-start | bytes 776 | tf_op jit(solution)/shard_map/ppermute | solution.py:29
  118.1 12.2 %copy-start.1 = (f32[1,4096]{1,0:T(1,128)S(1)}, f32[1,4096]{1,0:T(1,128)}, u32[]{:S(2)}) copy-start(f32[1,4096]{1,0:T(1,128)} %param.8) | copy-start | bytes 49156
  148.6 51.7 %copy-start = (bf16[1,4096,128]{1,2,0:T(8,128)(2,1)S(1)}, bf16[1,4096,128]{1,2,0:T(8,128)(2,1)}, u32[]{:S(2)}) copy-start(bf16[1,4096,128]{1,2,0:T(8,128)(2,1)} %copy.25) | copy-start | bytes 3145732
  161.3 24.0 %all-to-all-start.1 = ((f32[16,2,128]{2,1,0:T(2,128)}), f32[16,2,128]{2,1,0:T(2,128)S(1)}, u32[]{:S(2)}, u32[]{:S(2)}) async-start(f32[16,2,128]{2,1,0:T(2,128)} %broadcast_in_dim.19), calls=%async_computation.1 | async-start | bytes 32768 | tf_op jit(solution)/shard_map/all_to_all | solution.py:33
  185.9 12.7 %all-to-all-start.2 = ((f32[32,2,128]{2,1,0:T(2,128)}), f32[32,2,128]{2,1,0:T(2,128)S(1)}, u32[]{:S(2)}, u32[]{:S(2)}) async-start(f32[32,2,128]{2,1,0:T(2,128)} %broadcast_in_dim.20), calls=%async_computation.2 | async-start | bytes 65536 | tf_op jit(solution)/shard_map/all_to_all | solution.py:33
  229.5 12.5 %all-to-all-start.5 = ((f32[32,2,128]{2,1,0:T(2,128)}), f32[32,2,128]{2,1,0:T(2,128)S(1)}, u32[]{:S(2)}, u32[]{:S(2)}) async-start(f32[32,2,128]{2,1,0:T(2,128)} %broadcast_in_dim.23), calls=%async_computation.5 | async-start | bytes 65536 | tf_op jit(solution)/shard_map/all_to_all | solution.py:33

commit v2 on v1

v2 whole, which is shorter than its diff:
```python
import math

import jax
import jax.numpy as jnp
import numpy as np
from jax import lax
from jax.experimental import pallas as pl
from jax.experimental.pallas import tpu as pltpu
from jax.sharding import Mesh, PartitionSpec as P


AXES = ("zh", "x", "y", "zl", "core")
AXIS_SIZES = (4, 4, 4, 4, 2)
KX = ("zh", "x")
KY = ("y", "zl", "core")
PLANE = ("x", "y", "core")
COLUMN = ("zh", "zl")

GX = 64
GY = 64
NQ = 2
GRID = GX * GY
BANDS = 128
LANES = 128
ROWS = GRID // LANES
STEP = 512

SMEAR = 0.5
FERMI = 0.0
SCREEN = 4.0


def hartley_table(length):
    positions = np.arange(length)
    angles = positions[:, None] * positions[None, :] % length * (2.0 * math.pi / length)
    return (np.cos(angles) + np.sin(angles)) / math.sqrt(length)


def screening(len_x, len_y):
    freq_x = np.arange(len_x)
    freq_x = np.minimum(freq_x, len_x - freq_x)
    freq_y = np.arange(len_y)
    freq_y = np.minimum(freq_y, len_y - freq_y)
    return 1.0 / (1.0 + (freq_x[:, None] ** 2 + freq_y[None, :] ** 2) / SCREEN)


def lane_block(index):
    return pl.ds(pl.multiple_of(index * LANES, LANES), LANES)


def in_parts(value):
    high = value.astype(jnp.bfloat16)
    rest = value - high.astype(jnp.float32)
    middle = rest.astype(jnp.bfloat16)
    low = (rest - middle.astype(jnp.float32)).astype(jnp.bfloat16)
    return (high, middle, low)


def occupation(energy):
    return 1.0 / (1.0 + jnp.exp((energy - FERMI) / SMEAR))


def across(row):
    return jnp.broadcast_to(row, (BANDS, BANDS)).T


def weights(energy, far_energy):
    energy = energy.astype(jnp.float32)
    far_energy = far_energy.astype(jnp.float32)
    gap = far_energy - across(energy)
    filled = across(occupation(energy)) - occupation(far_energy)
    return filled * gap / (gap * gap + SMEAR * SMEAR)


def weigh(potential_ref, own_ref, weighted_ref):
    for block in range(ROWS):
        at = slice(block * LANES, (block + 1) * LANES)
        product = potential_ref[block : block + 1, :] * own_ref[:, at].astype(jnp.float32)
        weighted_ref[:, at] = product.astype(jnp.bfloat16)


def respond(weighted_ref, far_ref, own_ref, weight, terms_ref):
    bands = jnp.zeros((BANDS, BANDS), jnp.float32)
    for start in range(0, GRID, STEP):
        at = slice(start, start + STEP)
        bands += jnp.dot(weighted_ref[:, at], far_ref[at, :], preferred_element_type=jnp.float32)
    response = weight * (bands * (1.0 / math.sqrt(GRID)))
    low = response.astype(jnp.bfloat16)
    for start in range(0, GRID, STEP):
        at = slice(start, start + STEP)
        orbitals = lax.dot_general(
            low, far_ref[at, :], (((1,), (1,)), ((), ())), preferred_element_type=jnp.float32
        )
        term = jnp.sum(own_ref[:, at].astype(jnp.float32) * orbitals, axis=0, keepdims=True)
        term = term * (1.0 / math.sqrt(BANDS))
        for block in range(STEP // LANES):
            row = start // LANES + block
            terms_ref[row : row + 1, :] = term[:, block * LANES : (block + 1) * LANES]
    return response


def to_far_order(value_ref, order_ref, column_ref, parts_ref):
    parts = in_parts(value_ref[...])
    rows = lax.broadcasted_iota(jnp.int32, (ROWS, LANES), 0)
    for block in range(ROWS):
        mine = (order_ref[block : block + 1, :] // LANES) == rows
        at = slice(block * LANES, (block + 1) * LANES)
        for index, part in enumerate(parts):
            wide = part[block : block + 1, :].astype(jnp.float32)
            parts_ref[index * ROWS : (index + 1) * ROWS, at] = jnp.where(mine, wide, 0.0).astype(jnp.bfloat16)
    sums = lax.dot_general(
        parts_ref[...], column_ref[...], (((1,), (1,)), ((), ())), preferred_element_type=jnp.float32
    )
    return sums[:ROWS] + sums[ROWS : 2 * ROWS] + sums[2 * ROWS :]


def from_far_order(value, order_ref, column_ref, out_ref, first_row):
    stacked = jnp.concatenate([part.astype(jnp.float32) for part in in_parts(value)]).astype(jnp.bfloat16)
    rows = lax.broadcasted_iota(jnp.int32, (ROWS, LANES), 0)
    for start in range(0, GRID, STEP):
        at = slice(start, start + STEP)
        spread = jnp.dot(stacked, column_ref[:, at], preferred_element_type=jnp.float32)
        spread = spread[:ROWS] + spread[ROWS : 2 * ROWS] + spread[2 * ROWS :]
        for block in range(STEP // LANES):
            row = start // LANES + block
            mine = (order_ref[row : row + 1, :] // LANES) == rows
            picked = jnp.where(mine, spread[:, block * LANES : (block + 1) * LANES], 0.0)
            out_ref[first_row + row : first_row + row + 1, :] = jnp.sum(picked, axis=0, keepdims=True)


UNROLL = 32


def prepare_kernel(order_smem, own_ref, order_ref, external_ref,
                   turned_ref, moved_ref, weighted_ref, column_ref, wide, scattered, parts, potential):
    wide[...] = own_ref[...].astype(jnp.float32)

    def move(step, carry):
        base = step * UNROLL
        for offset in range(UNROLL):
            row = base + offset
            scattered[pl.ds(order_smem[row], 1), :] = wide[pl.ds(row, 1), :]
        return carry

    lax.fori_loop(0, GRID // UNROLL, move, 0)
    columns = lax.broadcasted_iota(jnp.int32, (LANES, LANES), 0)

    def turn(block, carry):
        at = lane_block(block)
        turned_ref[:, at] = wide[at, :].T.astype(jnp.bfloat16)
        moved_ref[:, at] = scattered[at, :].T.astype(jnp.bfloat16)
        mine = (order_ref[pl.ds(block, 1), :] % LANES) == columns
        column_ref[:, at] = jnp.where(mine, 1.0, 0.0).astype(jnp.bfloat16)
        return carry

    lax.fori_loop(0, ROWS, turn, 0)
    potential[...] = to_far_order(external_ref, order_ref, column_ref, parts)
    weigh(potential, moved_ref, weighted_ref)


def second_kernel(order_smem, sent_ref, turned_ref, external_ref, energy_ref, far_energy_ref,
                  far_ref, terms_ref, wide, gathered, weighted):
    wide[...] = sent_ref[...].astype(jnp.float32)

    def move(step, carry):
        base = step * UNROLL
        for offset in range(UNROLL):
            row = base + offset
            gathered[pl.ds(row, 1), :] = wide[pl.ds(order_smem[row], 1), :]
        return carry

    lax.fori_loop(0, GRID // UNROLL, move, 0)
    far_ref[...] = gathered[...].astype(jnp.bfloat16)
    weigh(external_ref, turned_ref, weighted)
    respond(weighted, far_ref, turned_ref, weights(energy_ref[...], far_energy_ref[...]), terms_ref)


def first_kernel(flag_smem, *refs):
    piece_refs = refs[:4]
    (beside_ref, moved_ref, weighted_ref, order_ref, column_ref, energy_ref, far_energy_ref, other_ref,
     far_ref, terms_ref, own_terms) = refs[4:]

    @pl.when(flag_smem[0] == 1)
    def _():
        start = 0
        for piece in piece_refs:
            far_ref[start : start + piece.shape[0], :] = piece[...]
            start += piece.shape[0]

    @pl.when(flag_smem[0] == 0)
    def _():
        far_ref[...] = beside_ref[...]

    respond(weighted_ref, far_ref, moved_ref, weights(energy_ref[...], far_energy_ref[...]), own_terms)
    from_far_order(own_terms[...], order_ref, column_ref, terms_ref, 0)
    terms_ref[ROWS:, :] = other_ref[...]


def exact_dot(left, right):
    return jnp.dot(left, right, precision=lax.Precision.HIGHEST, preferred_element_type=jnp.float32)


def last_kernel(density_ref, external_ref, even_ref, odd_ref, into_ref, back_ref, screen_ref, even_t_ref, odd_t_ref,
                first_ref, second_ref, moved_ref, turned_ref, order_ref, column_ref,
                energy_ref, first_energy_ref, second_energy_ref,
                response_ref, terms_ref, parts, potential, moved_potential, weighted, own_terms):
    scale = 1.0 / math.sqrt(math.prod(AXIS_SIZES))
    low_half = lax.broadcasted_iota(jnp.int32, (ROWS, LANES), 1) < GY
    along_y = exact_dot(density_ref[...] * scale, into_ref[...])
    for q_index in range(NQ):
        at = slice(q_index * ROWS, (q_index + 1) * ROWS)
        spectrum = exact_dot(even_ref[...], along_y[at, :LANES]) + exact_dot(odd_ref[...], along_y[at, LANES:])
        back = exact_dot(spectrum * screen_ref[...], back_ref[...])
        field = jnp.where(low_half, exact_dot(even_t_ref[...], back), exact_dot(odd_t_ref[...], back))
        potential[at, :] = external_ref[...] + field
    moved_potential[...] = to_far_order(potential.at[0:ROWS], order_ref, column_ref, parts)
    weigh(moved_potential, moved_ref, weighted)
    weight = weights(energy_ref[...], first_energy_ref[...])
    response_ref[0] = respond(weighted, first_ref, moved_ref, weight, own_terms).T
    from_far_order(own_terms[...], order_ref, column_ref, terms_ref, 0)
    weigh(potential.at[ROWS : 2 * ROWS], turned_ref, weighted)
    weight = weights(energy_ref[...], second_energy_ref[...])
    response_ref[1] = respond(weighted, second_ref, turned_ref, weight, own_terms).T
    terms_ref[ROWS:, :] = own_terms[...]


def coulomb_tables():
    table = hartley_table(GX)
    other = hartley_table(GY)
    none = np.zeros((GY, 2 * GY))
    twice = np.concatenate([other, other], axis=1)
    into = np.concatenate([np.concatenate([twice, none]), np.concatenate([none, twice])], axis=1)
    back = np.concatenate([twice, none])
    screen = screening(GX, GY)
    screen = np.concatenate([screen, screen], axis=1)
    even, odd = table[:, 0::2], table[:, 1::2]
    return [part.astype(np.float32) for part in (even, odd, into, back, screen, even.T, odd.T)]


VMEM = pl.BlockSpec(memory_space=pltpu.VMEM)
SMEM = pl.BlockSpec(memory_space=pltpu.SMEM)


def local_call(kernel, smem, arrays, outs, scratch, microseconds):
    return pl.pallas_call(
        kernel,
        out_shape=[jax.ShapeDtypeStruct(shape, kind) for shape, kind in outs],
        in_specs=[SMEM] * smem + [VMEM] * (len(arrays) - smem),
        out_specs=[VMEM] * len(outs),
        scratch_shapes=[pltpu.VMEM(shape, kind) for shape, kind in scratch],
        cost_estimate=pl.CostEstimate(flops=0, bytes_accessed=microseconds * 3000000, transcendentals=0),
    )(*arrays)


F32 = jnp.float32
BF16 = jnp.bfloat16
TALL = (GRID, BANDS)
TURNED = (BANDS, GRID)
BLOCKS = (ROWS, LANES)


def prepare(order, own, order_blocks, external):
    return local_call(
        prepare_kernel, 1, (order, own, order_blocks, external),
        [(TURNED, BF16)] * 3 + [((LANES, GRID), BF16)],
        [(TALL, F32), (TALL, F32), ((3 * ROWS, GRID), BF16), (BLOCKS, F32)], 12,
    )


def second_round_one(order, sent, turned, external, energy, far_energy):
    return local_call(
        second_kernel, 1, (order, sent, turned, external, energy, far_energy),
        [(TALL, BF16), (BLOCKS, F32)], [(TALL, F32), (TALL, F32), (TURNED, BF16)], 12,
    )


def first_round_one(flag, pieces, beside, moved, weighted, order_blocks, column, energy, far_energy, other):
    arrays = (flag, *pieces, beside, moved, weighted, order_blocks, column, energy, far_energy, other)
    return local_call(first_kernel, 1, arrays, [(TALL, BF16), ((2 * ROWS, LANES), F32)], [(BLOCKS, F32)], 3)


def round_two(density, external, first, second, moved, turned, order_blocks, column, energy, first_energy, second_energy):
    arrays = (density, external, *[jnp.asarray(part) for part in coulomb_tables()], first, second, moved, turned,
              order_blocks, column, energy, first_energy, second_energy)
    return local_call(
        last_kernel, 0, arrays,
        [((NQ, BANDS, BANDS), F32), ((2 * ROWS, LANES), F32)],
        [((3 * ROWS, GRID), BF16), ((2 * ROWS, LANES), F32), (BLOCKS, F32), (TURNED, BF16), (BLOCKS, F32)], 5,
    )


def exchange(value, axes):
    return lax.all_to_all(value, axes, 0, 0, tiled=True)


def summed_everywhere(value):
    plane = lax.axis_size(PLANE)
    column = lax.axis_size(COLUMN)
    chunks = value.reshape(plane, -1, LANES)
    part = jnp.sum(exchange(chunks, PLANE), axis=0)
    copies = jnp.broadcast_to(part[None], (column,) + part.shape)
    part = jnp.sum(exchange(copies, COLUMN), axis=0)
    copies = jnp.broadcast_to(part[None], (plane,) + part.shape)
    return exchange(copies, PLANE).reshape(value.shape)


def next_along(value, axis):
    count = lax.axis_size(axis)
    return lax.ppermute(value, axis, [(source, (source - 1) % count) for source in range(count)])


def iterate(states, energies, external, reorder):
    orbital = states[0]
    external = external.reshape(BLOCKS)
    order_blocks = reorder[0, 0].reshape(BLOCKS)
    column_index = lax.axis_index("x")

    outer = GRID * 5 // 16
    inner = GRID // 2 - outer
    cuts = (0, outer, outer + inner, outer + 2 * inner, GRID)
    parts = [orbital[cuts[c] : cuts[c + 1]] for c in range(4)]
    spread = [lax.ppermute(parts[c], "x", [(0, c)]) for c in range(1, 4)]
    far_second = next_along(orbital, KY)
    beside = lax.ppermute(orbital, "x", [(1, 0), (2, 1), (3, 2)])
    wide = jnp.where(column_index == 0, parts[0], spread[2])
    narrow = jnp.where(column_index == 1, spread[0], spread[1])
    wide, narrow, own = lax.optimization_barrier((wide, narrow, orbital))
    count = lax.axis_size("zh")
    hops = [(source, (source - 1) % count) for source in range(count)]
    wide = lax.ppermute(wide, KX, [(4 * s + x, 4 * t + x) for s, t in hops for x in (0, 3)])
    narrow = lax.ppermute(narrow, KX, [(4 * s + x, 4 * t + x) for s, t in hops for x in (1, 2)])
    second_energy = next_along(energies, KY)
    first_energy = next_along(energies, KX)

    turned, moved, weighted, column = prepare(reorder[0, 0], own, order_blocks, external)
    second_states, second_terms = second_round_one(
        reorder[1, 0], far_second, turned, external, energies, second_energy
    )

    second_terms, wide, narrow = lax.optimization_barrier((second_terms, wide, narrow))
    pieces = [lax.ppermute(wide, "x", [(0, 3)])]
    pieces += [lax.ppermute(narrow, "x", [(x, 3)]) for x in (1, 2)]
    flag = (column_index == 3).astype(jnp.int32).reshape(1)
    first_states, terms = first_round_one(
        flag, pieces + [wide], beside, moved, weighted, order_blocks, column, energies, first_energy, second_terms
    )
    response, terms = round_two(
        summed_everywhere(terms), external, first_states, second_states, moved, turned, order_blocks, column,
        energies, first_energy, second_energy,
    )
    density = summed_everywhere(terms) * (1.0 / math.sqrt(lax.axis_size(AXES)))
    return (response.reshape(1, NQ, 1, BANDS, BANDS), density.reshape(NQ, 1, GRID))


def solution(mesh):
    fine = Mesh(mesh.devices.reshape(AXIS_SIZES), AXES)
    return jax.shard_map(
        iterate,
        mesh=fine,
        in_specs=(
            P(AXES, None, None),
            P(AXES, None),
            P(),
            P(None, AXES, None),
        ),
        out_specs=(P(AXES, None, None, None, None), P()),
        check_vma=False,
    )
```

time: 243 us -> 180 us (0.74)
  waiting for transfers between devices: 112 us -> 3.84 us
  blocking collectives: 36.5 us -> 87.7 us
  Pallas kernels: 0 us -> 29.7 us
  local copies, waits for them, and re-layouts: 30.2 us -> 6.65 us
  matrix products: 11.3 us -> 0 us
  starting transfers between devices: 49.5 us -> 47 us
    ppermute x4 -> x12, waiting for transfers between devices: 86.5 us -> 3.84 us  [the longest x1 2.08 us: iterate(): lax.ppermute(wide, KX, [(4 * s + x, 4 * t + x) for s, t in hops for x in...]
    all_to_all x3 -> x6, blocking collectives: 36.5 us -> 87.7 us  [exchange(): return lax.all_to_all(value, axes, 0, 0, tiled=True)]
    pallas_call x0 -> x4, Pallas kernels: none -> 29.7 us  [local_call(): pl.pallas_call(kernel, out_shape=[jax.ShapeDtypeStruct(shape, kind) for s...]
    all_to_all x3 -> x0, waiting for transfers between devices: 25.3 us -> none  [exchange(): return lax.all_to_all(value, axes, 0, 0, tiled=True)]
    gather x2 -> x0, local copies, waits for them, and re-layouts: 24.3 us -> none  [partner_of(): return (jnp.take(far_states, reorder[q_index, 0], axis=0), far_energy)]
    all_to_all x3 -> x0, starting transfers between devices: 23 us -> none  [exchange(): return lax.all_to_all(value, axes, 0, 0, tiled=True)]
    ppermute x4 -> x12, starting transfers between devices: 26.5 us -> 47 us  [the longest x3 18.3 us: next_along(): lax.ppermute(value, axis, [(source, (source - 1) % count) for source in r...]
    dot_general x10 -> x0, matrix products: 11.3 us -> none  [the longest x4 8.27 us: respond(): jnp.einsum('gm,amn->agn', far_states, response_low, preferred_element_typ...]
  transfers between devices with their start and end apart: 7 -> 12, of which waited for: 5 -> 3; matrix products, arithmetic and copies ran while one was open for 8% -> 3% of each run, Pallas kernels for 0% -> 10%
where the time goes in v2:
time: 180 us; the launch traced here: 179 us
  blocking collectives  87.7 us (49%)
  starting transfers between devices  47 us (26%)
  Pallas kernels  29.7 us (16%)
  local copies, waits for them, and re-layouts  6.65 us (4%)
  waiting for transfers between devices  3.84 us (2%)
  other arithmetic  3.19 us (2%)
    all_to_all x6, blocking collectives, exchange(): return lax.all_to_all(value, axes, 0, 0, tiled=True)  87.7 us
    pallas_call x4, Pallas kernels, local_call(): pl.pallas_call(kernel, out_shape=[jax.ShapeDtypeStruct(shape, kind) for s...  29.7 us
    ppermute x3, starting transfers between devices, next_along(): lax.ppermute(value, axis, [(source, (source - 1) % count) for source in r...  18.3 us
    ppermute x1, starting transfers between devices, iterate(): lax.ppermute(wide, KX, [(4 * s + x, 4 * t + x) for s, t in hops for x in...  9.75 us
    ppermute x3, starting transfers between devices, iterate(): spread = [lax.ppermute(parts[c], 'x', [(0, c)]) for c in range(1, 4)]  9.41 us
    ppermute x1, starting transfers between devices, iterate(): pieces = [lax.ppermute(wide, 'x', [(0, 3)])]  5.56 us
    slice x2, local copies, waits for them, and re-layouts, iterate(): parts = [orbital[cuts[c]:cuts[c + 1]] for c in range(4)]  3.6 us
  transfers between devices with their start and end apart: 12, of which 3 were waited for; matrix products, arithmetic and copies ran while one was open for 3% of the time, Pallas kernels for 10%

profile of v2, /device:TPU:1, one launch (start us, length us, event | category | flops | bytes accessed | tf_op | source)
XLA Modules:
  0.0 179.0 jit_solution(14498601382023026004)
XLA Ops:
  0.6 1.9 %slice_bitcast_fusion.1 = (bf16[768,128]{1,0:T(8,128)(2,1)}, bf16[768,128]{1,0:T(8,128)(2,1)}) fusion(bf16[1,4096,128]{2,1,0:T(8,128)(2,1)} %param.11), kind=kLoop, calls=%fused_computation.2 | loop fusion | bytes 786432 | tf_op jit(solution)/shard_map/slice | solution.py:321
  2.5 6.2 %collective-permute-start.3 = (bf16[768,128]{1,0:T(8,128)(2,1)}, bf16[768,128]{1,0:T(8,128)(2,1)}, u32[]{:S(2)}, u32[]{:S(2)}) collective-permute-start(bf16[768,128]{1,0:T(8,128)(2,1)} %get-tuple-element.40), channel_id=1, source_target_pairs={{0,64},{1,65},{2,66},{3,67},{4,68},{5,69},{6,70},{7,71},{8,72},{9,... | collective-permute-start | bytes 589832 | tf_op jit(solution)/shard_map/ppermute | solution.py:322
  8.7 2.0 %collective-permute-start.2 = (bf16[768,128]{1,0:T(8,128)(2,1)}, bf16[768,128]{1,0:T(8,128)(2,1)}, u32[]{:S(2)}, u32[]{:S(2)}) collective-permute-start(bf16[768,128]{1,0:T(8,128)(2,1)} %get-tuple-element.41), channel_id=1, source_target_pairs={{0,32},{1,33},{2,34},{3,35},{4,36},{5,37},{6,38},{7,39},{8,40},{9,... | collective-permute-start | bytes 589832 | tf_op jit(solution)/shard_map/ppermute | solution.py:322
  10.6 1.7 slice_bitcast_fusion
  12.4 1.3 collective-permute-start.1
  13.7 1.3 collective-permute-start.10
  15.0 4.6 %collective-permute-start = (bf16[4096,128]{1,0:T(8,128)(2,1)S(1)}, bf16[4096,128]{1,0:T(8,128)(2,1)S(1)}, u32[]{:S(2)}, u32[]{:S(2)}) collective-permute-start(bf16[4096,128]{1,0:T(8,128)(2,1)S(1)} %bitcast.23), channel_id=1, source_target_pairs={{0,31},{1,0},{2,1},{3,2},{4,3},{5,4},{6,5},{7,6},{8,7},{9,8},{10,9... | collective-permute-start | bytes 3145736 | tf_op jit(solution)/shard_map/ppermute | solution.py:309
  20.2 6.4 %collective-permute-start.4 = (bf16[1,128]{1,0:T(2,128)(2,1)S(1)}, bf16[1,128]{1,0:T(2,128)(2,1)S(1)}, u32[]{:S(2)}, u32[]{:S(2)}) collective-permute-start(bf16[1,128]{1,0:T(2,128)(2,1)S(1)} %copy-done.8), channel_id=1, source_target_pairs={{0,31},{1,0},{2,1},{3,2},{4,3},{5,4},{6,5},{7,6},{8,7},{9,8},{10,9... | collective-permute-start | bytes 776 | tf_op jit(solution)/shard_map/ppermute | solution.py:309
  26.7 1.6 broadcast_select_fusion
  29.1 1.3 collective-permute-start.6
  30.4 9.7 %collective-permute-start.5 = (bf16[1280,128]{1,0:T(8,128)(2,1)}, bf16[1280,128]{1,0:T(8,128)(2,1)S(1)}, u32[]{:S(2)}, u32[]{:S(2)}) collective-permute-start(bf16[1280,128]{1,0:T(8,128)(2,1)} %bitcast_select_fusion), channel_id=1, source_target_pairs={{0,384},{96,480},{128,0},{224,96},{256,128},{352,224},{384,256},{4... | collective-permute-start | bytes 983048 | tf_op jit(solution)/shard_map/ppermute | solution.py:330
  40.8 10.6 %shard_map.122 = (bf16[128,4096]{1,0:T(8,128)(2,1)}, bf16[128,4096]{1,0:T(8,128)(2,1)}, bf16[128,4096]{1,0:T(8,128)(2,1)}, bf16[128,4096]{1,0:T(8,128)(2,1)}) custom-call(s32[4096]{0:T(1024)} %bitcast.24, bf16[4096,128]{1,0:T(8,128)(2,1)} %bitcast.21, s32[32,128]{1,0:T(8,128)} %bitcast.25, f32[32,128]{1,0:T(8,128)} %bitcast.28), custom_call_target="tpu_custom_call" | custom-call | bytes 36000000 | tf_op jit(solution)/shard_map/pallas_call | solution.py:245
  52.5 7.2 %shard_map.123 = (bf16[4096,128]{1,0:T(8,128)(2,1)}, f32[32,128]{1,0:T(8,128)}) custom-call(s32[4096]{0:T(1024)} %bitcast.32, bf16[4096,128]{1,0:T(8,128)(2,1)} %copy-done.1, bf16[128,4096]{1,0:T(8,128)(2,1)} %get-tuple-element.19.turned_ref, f32[32,128]{1,0:T(8,128)} %bitcast.29, bf16[1,128]{1,0:T(2,128)(2,1)} %energy_ref.3, bf16[1,128]{1,0:T(2,128)(2,1)} %copy-done.11), custom_call_target="tpu_custom_call" | custom-call | bytes 36000000 | tf_op jit(solution)/shard_map/pallas_call | solution.py:245
  59.7 2.1 %collective-permute-done.5.refs_3_ = bf16[1280,128]{1,0:T(8,128)(2,1)S(1)} collective-permute-done((bf16[1280,128]{1,0:T(8,128)(2,1)}, bf16[1280,128]{1,0:T(8,128)(2,1)S(1)}, u32[]{:S(2)}, u32[]{:S(2)}) %collective-permute-start.5) | collective-permute-done | bytes 327712 | tf_op jit(solution)/shard_map/ppermute | solution.py:330
  61.8 5.6 %collective-permute-start.7 = (bf16[1280,128]{1,0:T(8,128)(2,1)S(1)}, bf16[1280,128]{1,0:T(8,128)(2,1)S(1)}, u32[]{:S(2)}, u32[]{:S(2)}) collective-permute-start(bf16[1280,128]{1,0:T(8,128)(2,1)S(1)} %collective-permute-done.5.refs_3_), channel_id=1, source_target_pairs={{0,96},{1,97},{2,98},{3,99},{4,100},{5,101},{6,102},{7,103},{8,104... | collective-permute-start | bytes 983048 | tf_op jit(solution)/shard_map/ppermute | solution.py:341
  68.7 7.3 %collective-permute-start.11 = (bf16[1,128]{1,0:T(2,128)(2,1)S(1)}, bf16[1,128]{1,0:T(2,128)(2,1)S(1)}, u32[]{:S(2)}, u32[]{:S(2)}) collective-permute-start(bf16[1,128]{1,0:T(2,128)(2,1)S(1)} %copy-done.9), channel_id=1, source_target_pairs={{0,480},{32,0},{64,32},{96,64},{128,96},{160,128},{192,160},{224,1... | collective-permute-start | bytes 776 | tf_op jit(solution)/shard_map/ppermute | solution.py:309
  78.6 4.4 %shard_map.124 = (bf16[4096,128]{1,0:T(8,128)(2,1)}, f32[64,128]{1,0:T(8,128)}) custom-call(s32[1]{0:T(128)} %bitcast.flag_smem, bf16[1280,128]{1,0:T(8,128)(2,1)} %copy-done.4, bf16[768,128]{1,0:T(8,128)(2,1)} %copy-done.6, bf16[768,128]{1,0:T(8,128)(2,1)} %copy-done.5, bf16[1280,128]{1,0:T(8,128)(2,1)} %copy-done.3, bf16[4096,128]{1,0:T(8,128)(2,1)} %copy-done.2, ...), custom_call_target="tpu_custom_call" | custom-call | bytes 9000000 | tf_op jit(solution)/shard_map/pallas_call | solution.py:245
  83.0 17.2 %all_to_all.30 = f32[32,2,128]{2,1,0:T(2,128)S(1)} all-to-all(f32[32,2,128]{2,1,0:T(2,128)} %bitcast.34), channel_id=1, replica_groups=mesh['zh'=4,'x'=4,'y'=4,'zl'=4,'core'=2] {'x','y','core'}, dimensions={0} | all-to-all | bytes 65536 | tf_op jit(solution)/shard_map/all_to_all | solution.py:293
  100.3 21.0 %all_to_all.31 = f32[16,2,128]{2,1,0:T(2,128)S(1)} all-to-all(f32[16,2,128]{2,1,0:T(2,128)S(1)} %broadcast_in_dim.8), channel_id=1, replica_groups=mesh['zh'=4,'x'=4,'y'=4,'zl'=4,'core'=2] {'zh','zl'}, dimensions={0} | all-to-all | bytes 32768 | tf_op jit(solution)/shard_map/all_to_all | solution.py:293
  121.3 12.4 %all_to_all.32 = f32[32,2,128]{2,1,0:T(2,128)} all-to-all(f32[32,2,128]{2,1,0:T(2,128)S(1)} %broadcast_in_dim.9), channel_id=1, replica_groups=mesh['zh'=4,'x'=4,'y'=4,'zl'=4,'core'=2] {'x','y','core'}, dimensions={0} | all-to-all | bytes 65536 | tf_op jit(solution)/shard_map/all_to_all | solution.py:293
  133.8 7.4 %shard_map.125 = (f32[2,128,128]{2,1,0:T(8,128)}, f32[64,128]{1,0:T(8,128)}) custom-call(f32[64,128]{1,0:T(8,128)} %bitcast.31, f32[32,128]{1,0:T(8,128)} %bitcast.30, f32[64,32]{1,0:T(8,128)} %constant.30.clone.even_ref, f32[64,32]{1,0:T(8,128)} %constant.31.clone.odd_ref, f32[128,256]{1,0:T(8,128)} %constant.32.clone.into_ref, ...), custom_call_target="tpu_custom_call" | custom-call | bytes 15000000 | tf_op jit(solution)/shard_map/pallas_call | solution.py:245
  141.2 11.3 %all_to_all.33 = f32[32,2,128]{2,1,0:T(2,128)S(1)} all-to-all(f32[32,2,128]{2,1,0:T(2,128)} %bitcast.33), channel_id=1, replica_groups=mesh['zh'=4,'x'=4,'y'=4,'zl'=4,'core'=2] {'x','y','core'}, dimensions={0} | all-to-all | bytes 65536 | tf_op jit(solution)/shard_map/all_to_all | solution.py:293
  152.6 13.9 %all_to_all.34 = f32[16,2,128]{2,1,0:T(2,128)S(1)} all-to-all(f32[16,2,128]{2,1,0:T(2,128)S(1)} %broadcast_in_dim.10), channel_id=1, replica_groups=mesh['zh'=4,'x'=4,'y'=4,'zl'=4,'core'=2] {'zh','zl'}, dimensions={0} | all-to-all | bytes 32768 | tf_op jit(solution)/shard_map/all_to_all | solution.py:293
  166.4 11.9 %all_to_all.35 = f32[32,2,128]{2,1,0:T(2,128)S(1)} all-to-all(f32[32,2,128]{2,1,0:T(2,128)S(1)} %broadcast_in_dim.11), channel_id=1, replica_groups=mesh['zh'=4,'x'=4,'y'=4,'zl'=4,'core'=2] {'x','y','core'}, dimensions={0} | all-to-all | bytes 65536 | tf_op jit(solution)/shard_map/all_to_all | solution.py:293
  (48 shorter events, 7.7 us)
Async XLA Ops:
  0.6 13.0 %copy-start = (bf16[1,4096,128]{2,1,0:T(8,128)(2,1)S(1)}, bf16[1,4096,128]{2,1,0:T(8,128)(2,1)}, u32[]{:S(2)}) copy-start(bf16[1,4096,128]{2,1,0:T(8,128)(2,1)} %param.11) | copy-start | bytes 3145732
  2.5 17.1 %collective-permute-start.3 = (bf16[768,128]{1,0:T(8,128)(2,1)}, bf16[768,128]{1,0:T(8,128)(2,1)}, u32[]{:S(2)}, u32[]{:S(2)}) collective-permute-start(bf16[768,128]{1,0:T(8,128)(2,1)} %get-tuple-element.40), channel_id=1, source_target_pairs={{0,64},{1,65},{2,66},{3,67},{4,68},{5,69},{6,70},{7,71},{8,72},{9,... | collective-permute-start | bytes 589832 | tf_op jit(solution)/shard_map/ppermute | solution.py:322
  8.7 18.0 %collective-permute-start.2 = (bf16[768,128]{1,0:T(8,128)(2,1)}, bf16[768,128]{1,0:T(8,128)(2,1)}, u32[]{:S(2)}, u32[]{:S(2)}) collective-permute-start(bf16[768,128]{1,0:T(8,128)(2,1)} %get-tuple-element.41), channel_id=1, source_target_pairs={{0,32},{1,33},{2,34},{3,35},{4,36},{5,37},{6,38},{7,39},{8,40},{9,... | collective-permute-start | bytes 589832 | tf_op jit(solution)/shard_map/ppermute | solution.py:322
  12.4 15.9 %collective-permute-start.1 = (bf16[1280,128]{1,0:T(8,128)(2,1)}, bf16[1280,128]{1,0:T(8,128)(2,1)S(1)}, u32[]{:S(2)}, u32[]{:S(2)}) collective-permute-start(bf16[1280,128]{1,0:T(8,128)(2,1)} %slice_bitcast_fusion), channel_id=1, source_target_pairs={{0,96},{1,97},{2,98},{3,99},{4,100},{5,101},{6,102},{7,103},{8,104... | collective-permute-start | bytes 983048 | tf_op jit(solution)/shard_map/ppermute | solution.py:322
  13.7 63.1 %collective-permute-start.10 = (bf16[4096,128]{1,0:T(8,128)(2,1)S(1)}, bf16[4096,128]{1,0:T(8,128)(2,1)S(1)}, u32[]{:S(2)}, u32[]{:S(2)}) collective-permute-start(bf16[4096,128]{1,0:T(8,128)(2,1)S(1)} %bitcast.22), channel_id=1, source_target_pairs={{32,0},{64,32},{96,64},{33,1},{65,33},{97,65},{34,2},{66,34},{98,6... | collective-permute-start | bytes 3145736 | tf_op jit(solution)/shard_map/ppermute | solution.py:324
  15.0 36.5 %collective-permute-start = (bf16[4096,128]{1,0:T(8,128)(2,1)S(1)}, bf16[4096,128]{1,0:T(8,128)(2,1)S(1)}, u32[]{:S(2)}, u32[]{:S(2)}) collective-permute-start(bf16[4096,128]{1,0:T(8,128)(2,1)S(1)} %bitcast.23), channel_id=1, source_target_pairs={{0,31},{1,0},{2,1},{3,2},{4,3},{5,4},{6,5},{7,6},{8,7},{9,8},{10,9... | collective-permute-start | bytes 3145736 | tf_op jit(solution)/shard_map/ppermute | solution.py:309
  19.6 0.7 copy-start.8
  20.2 31.2 %collective-permute-start.4 = (bf16[1,128]{1,0:T(2,128)(2,1)S(1)}, bf16[1,128]{1,0:T(2,128)(2,1)S(1)}, u32[]{:S(2)}, u32[]{:S(2)}) collective-permute-start(bf16[1,128]{1,0:T(2,128)(2,1)S(1)} %copy-done.8), channel_id=1, source_target_pairs={{0,31},{1,0},{2,1},{3,2},{4,3},{5,4},{6,5},{7,6},{8,7},{9,8},{10,9... | collective-permute-start | bytes 776 | tf_op jit(solution)/shard_map/ppermute | solution.py:309
  28.3 11.9 %copy-start.7 = (s32[2,1,4096]{2,1,0:T(1,128)S(1)}, s32[2,1,4096]{2,1,0:T(1,128)}, u32[]{:S(2)}) copy-start(s32[2,1,4096]{2,1,0:T(1,128)} %param.14) | copy-start | bytes 98308
  29.1 30.6 %collective-permute-start.6 = (bf16[768,128]{1,0:T(8,128)(2,1)}, bf16[768,128]{1,0:T(8,128)(2,1)}, u32[]{:S(2)}, u32[]{:S(2)}) collective-permute-start(bf16[768,128]{1,0:T(8,128)(2,1)} %broadcast_select_fusion), channel_id=1, source_target_pairs={{32,416},{64,448},{160,32},{192,64},{288,160},{320,192},{416,288},... | collective-permute-start | bytes 589832 | tf_op jit(solution)/shard_map/ppermute | solution.py:331
  30.4 31.4 %collective-permute-start.5 = (bf16[1280,128]{1,0:T(8,128)(2,1)}, bf16[1280,128]{1,0:T(8,128)(2,1)S(1)}, u32[]{:S(2)}, u32[]{:S(2)}) collective-permute-start(bf16[1280,128]{1,0:T(8,128)(2,1)} %bitcast_select_fusion), channel_id=1, source_target_pairs={{0,384},{96,480},{128,0},{224,96},{256,128},{352,224},{384,256},{4... | collective-permute-start | bytes 983048 | tf_op jit(solution)/shard_map/ppermute | solution.py:330
  51.5 0.5 copy-start.11
  51.5 1.0 copy-start.1
  59.7 9.0 %copy-start.9 = (bf16[1,128]{1,0:T(2,128)(2,1)S(1)}, bf16[1,128]{1,0:T(2,128)(2,1)}, u32[]{:S(2)}) copy-start(bf16[1,128]{1,0:T(2,128)(2,1)} %energy_ref.3) | copy-start | bytes 772
  61.8 16.1 %copy-start.3 = (bf16[1280,128]{1,0:T(8,128)(2,1)}, bf16[1280,128]{1,0:T(8,128)(2,1)S(1)}, u32[]{:S(2)}) copy-start(bf16[1280,128]{1,0:T(8,128)(2,1)S(1)} %collective-permute-done.5.refs_3_) | copy-start | bytes 983044
  61.8 16.1 %collective-permute-start.7 = (bf16[1280,128]{1,0:T(8,128)(2,1)S(1)}, bf16[1280,128]{1,0:T(8,128)(2,1)S(1)}, u32[]{:S(2)}, u32[]{:S(2)}) collective-permute-start(bf16[1280,128]{1,0:T(8,128)(2,1)S(1)} %collective-permute-done.5.refs_3_), channel_id=1, source_target_pairs={{0,96},{1,97},{2,98},{3,99},{4,100},{5,101},{6,102},{7,103},{8,104... | collective-permute-start | bytes 983048 | tf_op jit(solution)/shard_map/ppermute | solution.py:341
  67.4 9.4 %collective-permute-start.9 = (bf16[768,128]{1,0:T(8,128)(2,1)}, bf16[768,128]{1,0:T(8,128)(2,1)S(1)}, u32[]{:S(2)}, u32[]{:S(2)}) collective-permute-start(bf16[768,128]{1,0:T(8,128)(2,1)} %collective-permute-done.6), channel_id=1, source_target_pairs={{64,96},{65,97},{66,98},{67,99},{68,100},{69,101},{70,102},{71,103... | collective-permute-start | bytes 589832 | tf_op jit(solution)/shard_map/ppermute | solution.py:342
  68.0 8.8 %collective-permute-start.8 = (bf16[768,128]{1,0:T(8,128)(2,1)}, bf16[768,128]{1,0:T(8,128)(2,1)S(1)}, u32[]{:S(2)}, u32[]{:S(2)}) collective-permute-start(bf16[768,128]{1,0:T(8,128)(2,1)} %collective-permute-done.6), channel_id=1, source_target_pairs={{32,96},{33,97},{34,98},{35,99},{36,100},{37,101},{38,102},{39,103... | collective-permute-start | bytes 589832 | tf_op jit(solution)/shard_map/ppermute | solution.py:342
  68.7 8.0 %collective-permute-start.11 = (bf16[1,128]{1,0:T(2,128)(2,1)S(1)}, bf16[1,128]{1,0:T(2,128)(2,1)S(1)}, u32[]{:S(2)}, u32[]{:S(2)}) collective-permute-start(bf16[1,128]{1,0:T(2,128)(2,1)S(1)} %copy-done.9), channel_id=1, source_target_pairs={{0,480},{32,0},{64,32},{96,64},{128,96},{160,128},{192,160},{224,1... | collective-permute-start | bytes 776 | tf_op jit(solution)/shard_map/ppermute | solution.py:309
  76.8 1.1 copy-start.10
  76.8 1.1 copy-start.2
  76.8 1.1 copy-start.5
  76.8 1.1 copy-start.6
  77.9 0.7 copy-start.4

commit v3 on v2

--- a/solution.py
+++ b/solution.py
@@ -24,6 +24,7 @@
 LANES = 128
 ROWS = GRID // LANES
 STEP = 512
+LIMIT = 24 * 1024 * 1024
 
 SMEAR = 0.5
 FERMI = 0.0
@@ -249,6 +250,7 @@
         out_specs=[VMEM] * len(outs),
         scratch_shapes=[pltpu.VMEM(shape, kind) for shape, kind in scratch],
         cost_estimate=pl.CostEstimate(flops=0, bytes_accessed=microseconds * 3000000, transcendentals=0),
+        compiler_params=pltpu.CompilerParams(vmem_limit_bytes=LIMIT),
     )(*arrays)
 
 
@@ -315,20 +317,18 @@
     order_blocks = reorder[0, 0].reshape(BLOCKS)
     column_index = lax.axis_index("x")
 
-    outer = GRID * 5 // 16
-    inner = GRID // 2 - outer
-    cuts = (0, outer, outer + inner, outer + 2 * inner, GRID)
+    cuts = (0, 1456, 2160, 2864, GRID)
     parts = [orbital[cuts[c] : cuts[c + 1]] for c in range(4)]
+    count = lax.axis_size("zh")
+    hops = [(4 * source, 4 * ((source - 1) % count)) for source in range(count)]
+    hop0 = lax.ppermute(parts[0], KX, hops)
     spread = [lax.ppermute(parts[c], "x", [(0, c)]) for c in range(1, 4)]
     far_second = next_along(orbital, KY)
     beside = lax.ppermute(orbital, "x", [(1, 0), (2, 1), (3, 2)])
-    wide = jnp.where(column_index == 0, parts[0], spread[2])
-    narrow = jnp.where(column_index == 1, spread[0], spread[1])
-    wide, narrow, own = lax.optimization_barrier((wide, narrow, orbital))
-    count = lax.axis_size("zh")
-    hops = [(source, (source - 1) % count) for source in range(count)]
-    wide = lax.ppermute(wide, KX, [(4 * s + x, 4 * t + x) for s, t in hops for x in (0, 3)])
-    narrow = lax.ppermute(narrow, KX, [(4 * s + x, 4 * t + x) for s, t in hops for x in (1, 2)])
+    inner = jnp.where(column_index == 1, spread[0], spread[1])
+    outer, inner, own = lax.optimization_barrier((spread[2], inner, orbital))
+    hop3 = lax.ppermute(outer, KX, [(s + 3, t + 3) for s, t in hops])
+    hop12 = lax.ppermute(inner, KX, [(s + x, t + x) for s, t in hops for x in (1, 2)])
     second_energy = next_along(energies, KY)
     first_energy = next_along(energies, KX)
 
@@ -337,12 +337,12 @@
         reorder[1, 0], far_second, turned, external, energies, second_energy
     )
 
-    second_terms, wide, narrow = lax.optimization_barrier((second_terms, wide, narrow))
-    pieces = [lax.ppermute(wide, "x", [(0, 3)])]
-    pieces += [lax.ppermute(narrow, "x", [(x, 3)]) for x in (1, 2)]
+    second_terms, hop0, hop12, hop3 = lax.optimization_barrier((second_terms, hop0, hop12, hop3))
+    pieces = [lax.ppermute(hop0, "x", [(0, 3)])]
+    pieces += [lax.ppermute(hop12, "x", [(x, 3)]) for x in (1, 2)]
     flag = (column_index == 3).astype(jnp.int32).reshape(1)
     first_states, terms = first_round_one(
-        flag, pieces + [wide], beside, moved, weighted, order_blocks, column, energies, first_energy, second_terms
+        flag, pieces + [hop3], beside, moved, weighted, order_blocks, column, energies, first_energy, second_terms
     )
     response, terms = round_two(
         summed_everywhere(terms), external, first_states, second_states, moved, turned, order_blocks, column,

time: 180 us -> 188 us (1.044)
  local copies, waits for them, and re-layouts: 6.65 us -> 21.4 us
  waiting for transfers between devices: 3.84 us -> 11.7 us
  Pallas kernels: 29.7 us -> 23 us
  starting transfers between devices: 47 us -> 40.7 us
  other arithmetic: 3.19 us -> 0.8 us
    unnamed x24 -> x66, local copies, waits for them, and re-layouts: 2.39 us -> 19.3 us
    pallas_call x4, Pallas kernels: 29.7 us -> 23 us  [local_call(): pl.pallas_call(kernel, out_shape=[jax.ShapeDtypeStruct(shape, kind) for s...]
    ppermute x5 -> x6, waiting for transfers between devices: 3.13 us -> 9.35 us  [the longest x1 8.98 us: iterate(): hop0 = lax.ppermute(parts[0], KX, hops)]
    ppermute x5 -> x6, starting transfers between devices: 18 us -> 14.4 us  [the longest x1 9.76 us: iterate(): hop0 = lax.ppermute(parts[0], KX, hops)]
    ppermute x3, starting transfers between devices: 9.41 us -> 6.35 us  [iterate(): spread = [lax.ppermute(parts[c], 'x', [(0, c)]) for c in range(1, 4)]]
    select_n x2 -> x1, other arithmetic: 2.41 us -> 0.02 us  [iterate(): inner = jnp.where(column_index == 1, spread[0], spread[1])]
  transfers between devices with their start and end apart: 12 -> 13, of which waited for: 3 -> 3; matrix products, arithmetic and copies ran while one was open for 3% -> 1% of each run, Pallas kernels for 10% -> 8%
where the time goes in v3:
time: 188 us; the launch traced here: 187 us
  blocking collectives  88.1 us (47%)
  starting transfers between devices  40.7 us (22%)
  Pallas kernels  23 us (12%)
  local copies, waits for them, and re-layouts  21.4 us (11%)
  waiting for transfers between devices  11.7 us (6%)
    all_to_all x6, blocking collectives, exchange(): return lax.all_to_all(value, axes, 0, 0, tiled=True)  88.1 us
    pallas_call x4, Pallas kernels, local_call(): pl.pallas_call(kernel, out_shape=[jax.ShapeDtypeStruct(shape, kind) for s...  23 us
    unnamed x66, local copies, waits for them, and re-layouts  19.3 us
    ppermute x3, starting transfers between devices, next_along(): lax.ppermute(value, axis, [(source, (source - 1) % count) for source in r...  18.5 us
    ppermute x1, starting transfers between devices, iterate(): hop0 = lax.ppermute(parts[0], KX, hops)  9.76 us
    ppermute x1, waiting for transfers between devices, iterate(): hop0 = lax.ppermute(parts[0], KX, hops)  8.98 us
    ppermute x3, starting transfers between devices, iterate(): spread = [lax.ppermute(parts[c], 'x', [(0, c)]) for c in range(1, 4)]  6.35 us
  transfers between devices with their start and end apart: 13, of which 3 were waited for; matrix products, arithmetic and copies ran while one was open for 1% of the time, Pallas kernels for 8%

profile of v3, /device:TPU:1, one launch (start us, length us, event | category | flops | bytes accessed | tf_op | source)
XLA Modules:
  0.0 186.7 jit_solution(17076451354574101426)
XLA Ops:
  0.6 1.4 collective-permute-start.11
  2.1 8.8 %collective-permute-start = (bf16[4096,128]{1,0:T(8,128)(2,1)}, bf16[4096,128]{1,0:T(8,128)(2,1)}, u32[]{:S(2)}, u32[]{:S(2)}) collective-permute-start(bf16[4096,128]{1,0:T(8,128)(2,1)} %bitcast.22), channel_id=1, source_target_pairs={{0,31},{1,0},{2,1},{3,2},{4,3},{5,4},{6,5},{7,6},{8,7},{9,8},{10,9... | collective-permute-start | bytes 3145736 | tf_op jit(solution)/shard_map/ppermute | solution.py:311
  11.8 2.2 %collective-permute-start.1 = (bf16[1232,128]{1,0:T(8,128)(2,1)S(1)}, bf16[1232,128]{1,0:T(8,128)(2,1)}, u32[]{:S(2)}, u32[]{:S(2)}) collective-permute-start(bf16[1232,128]{1,0:T(8,128)(2,1)S(1)} %slice_bitcast_fusion.1), channel_id=1, source_target_pairs={{0,96},{1,97},{2,98},{3,99},{4,100},{5,101},{6,102},{7,103},{8,104... | collective-permute-start | bytes 946184 | tf_op jit(solution)/shard_map/ppermute | solution.py:325
  15.0 1.3 collective-permute-start.3
  16.4 2.9 %collective-permute-start.2 = (bf16[704,128]{1,0:T(8,128)(2,1)S(1)}, bf16[704,128]{1,0:T(8,128)(2,1)S(1)}, u32[]{:S(2)}, u32[]{:S(2)}) collective-permute-start(bf16[704,128]{1,0:T(8,128)(2,1)S(1)} %get-tuple-element.43), channel_id=1, source_target_pairs={{0,32},{1,33},{2,34},{3,35},{4,36},{5,37},{6,38},{7,39},{8,40},{9,... | collective-permute-start | bytes 540680 | tf_op jit(solution)/shard_map/ppermute | solution.py:325
  19.9 7.8 %collective-permute-start.4 = (bf16[1,128]{1,0:T(2,128)(2,1)S(1)}, bf16[1,128]{1,0:T(2,128)(2,1)S(1)}, u32[]{:S(2)}, u32[]{:S(2)}) collective-permute-start(bf16[1,128]{1,0:T(2,128)(2,1)S(1)} %copy-done.26), channel_id=1, source_target_pairs={{0,31},{1,0},{2,1},{3,2},{4,3},{5,4},{6,5},{7,6},{8,7},{9,8},{10,9... | collective-permute-start | bytes 776 | tf_op jit(solution)/shard_map/ppermute | solution.py:311
  27.8 9.8 %collective-permute-start.5 = (bf16[1456,128]{1,0:T(8,128)(2,1)S(1)}, bf16[1456,128]{1,0:T(8,128)(2,1)}, u32[]{:S(2)}, u32[]{:S(2)}) collective-permute-start(bf16[1456,128]{1,0:T(8,128)(2,1)S(1)} %slice_bitcast_fusion), channel_id=1, source_target_pairs={{0,384},{128,0},{256,128},{384,256},{1,385},{129,1},{257,129},{385... | collective-permute-start | bytes 1118216 | tf_op jit(solution)/shard_map/ppermute | solution.py:324
  37.6 1.3 collective-permute-start.6
  40.3 9.1 %shard_map.122 = (bf16[128,4096]{1,0:T(8,128)(2,1)S(1)}, bf16[128,4096]{1,0:T(8,128)(2,1)S(1)}, bf16[128,4096]{1,0:T(8,128)(2,1)S(1)}, bf16[128,4096]{1,0:T(8,128)(2,1)S(1)}) custom-call(s32[4096]{0:T(1024)S(1)} %bitcast.24, bf16[4096,128]{1,0:T(8,128)(2,1)S(1)} %bitcast.23, s32[32,128]{1,0:T(8,128)S(1)} %bitcast.25, f32[32,128]{1,0:T(8,128)S(1)} %bitcast.28), custom_call_target="tpu_custom_call" | custom-call | bytes 36000000 | tf_op jit(solution)/shard_map/pallas_call | solution.py:246
  50.4 6.6 %shard_map.123 = (bf16[4096,128]{1,0:T(8,128)(2,1)S(1)}, f32[32,128]{1,0:T(8,128)S(1)}) custom-call(s32[4096]{0:T(1024)S(1)} %bitcast.32, bf16[4096,128]{1,0:T(8,128)(2,1)} %collective-permute-done.sent_ref, bf16[128,4096]{1,0:T(8,128)(2,1)S(1)} %get-tuple-element.20.turned_ref, f32[32,128]{1,0:T(8,128)S(1)} %bitcast.29, bf16[1,128]{1,0:T(2,128)(2,1)S(1)} %copy-done.26, ...), custom_call_target="tpu_custom_call" | custom-call | bytes 36000000 | tf_op jit(solution)/shard_map/pallas_call | solution.py:246
  58.6 9.0 %collective-permute-done.5 = bf16[1456,128]{1,0:T(8,128)(2,1)} collective-permute-done((bf16[1456,128]{1,0:T(8,128)(2,1)S(1)}, bf16[1456,128]{1,0:T(8,128)(2,1)}, u32[]{:S(2)}, u32[]{:S(2)}) %collective-permute-start.5) | collective-permute-done | bytes 372768 | tf_op jit(solution)/shard_map/ppermute | solution.py:324
  68.3 1.3 collective-permute-start.8
  71.0 1.9 %collective-permute-start.12 = (bf16[1,128]{1,0:T(2,128)(2,1)S(1)}, bf16[1,128]{1,0:T(2,128)(2,1)S(1)}, u32[]{:S(2)}, u32[]{:S(2)}) collective-permute-start(bf16[1,128]{1,0:T(2,128)(2,1)S(1)} %copy-done.26), channel_id=1, source_target_pairs={{0,480},{32,0},{64,32},{96,64},{128,96},{160,128},{192,160},{224,1... | collective-permute-start | bytes 776 | tf_op jit(solution)/shard_map/ppermute | solution.py:311
  72.9 2.4 %collective-permute-done.12.refs_10_.first_energy_ref = bf16[1,128]{1,0:T(2,128)(2,1)S(1)} collective-permute-done((bf16[1,128]{1,0:T(2,128)(2,1)S(1)}, bf16[1,128]{1,0:T(2,128)(2,1)S(1)}, u32[]{:S(2)}, u32[]{:S(2)}) %collective-permute-start.12) | collective-permute-done | bytes 288 | tf_op jit(solution)/shard_map/ppermute | solution.py:311
  78.2 1.2 copy-done.2
  84.2 2.5 %shard_map.124 = (bf16[4096,128]{1,0:T(8,128)(2,1)S(1)}, f32[64,128]{1,0:T(8,128)S(1)}) custom-call(s32[1]{0:T(128)} %bitcast.flag_smem, bf16[1456,128]{1,0:T(8,128)(2,1)S(1)} %collective-permute-done.8.refs_0_, bf16[704,128]{1,0:T(8,128)(2,1)S(1)} %copy-done.15, bf16[704,128]{1,0:T(8,128)(2,1)S(1)} %copy-done.13, bf16[1232,128]{1,0:T(8,128)(2,1)S(1)} %copy-done.11, ...), custom_call_target="tpu_custom_call" | custom-call | bytes 9000000 | tf_op jit(solution)/shard_map/pallas_call | solution.py:246
  87.7 19.2 %all_to_all.30 = f32[32,2,128]{2,1,0:T(2,128)S(1)} all-to-all(f32[32,2,128]{2,1,0:T(2,128)S(1)} %bitcast.34), channel_id=1, replica_groups=mesh['zh'=4,'x'=4,'y'=4,'zl'=4,'core'=2] {'x','y','core'}, dimensions={0} | all-to-all | bytes 65536 | tf_op jit(solution)/shard_map/all_to_all | solution.py:295
  106.9 20.2 %all_to_all.31 = f32[16,2,128]{2,1,0:T(2,128)S(1)} all-to-all(f32[16,2,128]{2,1,0:T(2,128)S(1)} %broadcast_in_dim.8), channel_id=1, replica_groups=mesh['zh'=4,'x'=4,'y'=4,'zl'=4,'core'=2] {'zh','zl'}, dimensions={0} | all-to-all | bytes 32768 | tf_op jit(solution)/shard_map/all_to_all | solution.py:295
  127.2 12.1 %all_to_all.32 = f32[32,2,128]{2,1,0:T(2,128)S(1)} all-to-all(f32[32,2,128]{2,1,0:T(2,128)S(1)} %broadcast_in_dim.9), channel_id=1, replica_groups=mesh['zh'=4,'x'=4,'y'=4,'zl'=4,'core'=2] {'x','y','core'}, dimensions={0} | all-to-all | bytes 65536 | tf_op jit(solution)/shard_map/all_to_all | solution.py:295
  140.0 1.2 copy-done.5
  144.7 4.8 %shard_map.125 = (f32[2,128,128]{2,1,0:T(8,128)}, f32[64,128]{1,0:T(8,128)S(1)}) custom-call(f32[64,128]{1,0:T(8,128)S(1)} %bitcast.31, f32[32,128]{1,0:T(8,128)S(1)} %bitcast.30, f32[64,32]{1,0:T(8,128)S(1)} %copy-done.21, f32[64,32]{1,0:T(8,128)S(1)} %copy-done.20, f32[128,256]{1,0:T(8,128)S(1)} %copy-done.17, f32[128,128]{1,0:T(8,128)S(1)} %copy-done.18, ...), custom_call_target="tpu_custom_call" | custom-call | bytes 15000000 | tf_op jit(solution)/shard_map/pallas_call | solution.py:246
  149.5 10.7 %all_to_all.33 = f32[32,2,128]{2,1,0:T(2,128)S(1)} all-to-all(f32[32,2,128]{2,1,0:T(2,128)S(1)} %bitcast.33), channel_id=1, replica_groups=mesh['zh'=4,'x'=4,'y'=4,'zl'=4,'core'=2] {'x','y','core'}, dimensions={0} | all-to-all | bytes 65536 | tf_op jit(solution)/shard_map/all_to_all | solution.py:295
  160.3 13.9 %all_to_all.34 = f32[16,2,128]{2,1,0:T(2,128)S(1)} all-to-all(f32[16,2,128]{2,1,0:T(2,128)S(1)} %broadcast_in_dim.10), channel_id=1, replica_groups=mesh['zh'=4,'x'=4,'y'=4,'zl'=4,'core'=2] {'zh','zl'}, dimensions={0} | all-to-all | bytes 32768 | tf_op jit(solution)/shard_map/all_to_all | solution.py:295
  174.1 11.9 %all_to_all.35 = f32[32,2,128]{2,1,0:T(2,128)S(1)} all-to-all(f32[32,2,128]{2,1,0:T(2,128)S(1)} %broadcast_in_dim.11), channel_id=1, replica_groups=mesh['zh'=4,'x'=4,'y'=4,'zl'=4,'core'=2] {'x','y','core'}, dimensions={0} | all-to-all | bytes 65536 | tf_op jit(solution)/shard_map/all_to_all | solution.py:295
  (92 shorter events, 22.2 us)
Async XLA Ops:
  0.6 18.6 %copy-start = (bf16[1,4096,128]{2,1,0:T(8,128)(2,1)S(1)}, bf16[1,4096,128]{2,1,0:T(8,128)(2,1)}, u32[]{:S(2)}) copy-start(bf16[1,4096,128]{2,1,0:T(8,128)(2,1)} %param.11) | copy-start | bytes 3145732
  0.6 75.2 %collective-permute-start.11 = (bf16[4096,128]{1,0:T(8,128)(2,1)}, bf16[4096,128]{1,0:T(8,128)(2,1)}, u32[]{:S(2)}, u32[]{:S(2)}) collective-permute-start(bf16[4096,128]{1,0:T(8,128)(2,1)} %bitcast.21), channel_id=1, source_target_pairs={{32,0},{64,32},{96,64},{33,1},{65,33},{97,65},{34,2},{66,34},{98,6... | collective-permute-start | bytes 3145736 | tf_op jit(solution)/shard_map/ppermute | solution.py:327
  2.1 48.4 %collective-permute-start = (bf16[4096,128]{1,0:T(8,128)(2,1)}, bf16[4096,128]{1,0:T(8,128)(2,1)}, u32[]{:S(2)}, u32[]{:S(2)}) collective-permute-start(bf16[4096,128]{1,0:T(8,128)(2,1)} %bitcast.22), channel_id=1, source_target_pairs={{0,31},{1,0},{2,1},{3,2},{4,3},{5,4},{6,5},{7,6},{8,7},{9,8},{10,9... | collective-permute-start | bytes 3145736 | tf_op jit(solution)/shard_map/ppermute | solution.py:311
  11.8 25.7 %collective-permute-start.1 = (bf16[1232,128]{1,0:T(8,128)(2,1)S(1)}, bf16[1232,128]{1,0:T(8,128)(2,1)}, u32[]{:S(2)}, u32[]{:S(2)}) collective-permute-start(bf16[1232,128]{1,0:T(8,128)(2,1)S(1)} %slice_bitcast_fusion.1), channel_id=1, source_target_pairs={{0,96},{1,97},{2,98},{3,99},{4,100},{5,101},{6,102},{7,103},{8,104... | collective-permute-start | bytes 946184 | tf_op jit(solution)/shard_map/ppermute | solution.py:325
  15.0 4.3 %collective-permute-start.3 = (bf16[704,128]{1,0:T(8,128)(2,1)S(1)}, bf16[704,128]{1,0:T(8,128)(2,1)S(1)}, u32[]{:S(2)}, u32[]{:S(2)}) collective-permute-start(bf16[704,128]{1,0:T(8,128)(2,1)S(1)} %get-tuple-element.42), channel_id=1, source_target_pairs={{0,64},{1,65},{2,66},{3,67},{4,68},{5,69},{6,70},{7,71},{8,72},{9,... | collective-permute-start | bytes 540680 | tf_op jit(solution)/shard_map/ppermute | solution.py:325
  16.4 11.4 %collective-permute-start.2 = (bf16[704,128]{1,0:T(8,128)(2,1)S(1)}, bf16[704,128]{1,0:T(8,128)(2,1)S(1)}, u32[]{:S(2)}, u32[]{:S(2)}) collective-permute-start(bf16[704,128]{1,0:T(8,128)(2,1)S(1)} %get-tuple-element.43), channel_id=1, source_target_pairs={{0,32},{1,33},{2,34},{3,35},{4,36},{5,37},{6,38},{7,39},{8,40},{9,... | collective-permute-start | bytes 540680 | tf_op jit(solution)/shard_map/ppermute | solution.py:325
  19.3 20.3 %copy-start.32 = (s32[2,1,4096]{2,1,0:T(1,128)S(1)}, s32[2,1,4096]{2,1,0:T(1,128)}, u32[]{:S(2)}) copy-start(s32[2,1,4096]{2,1,0:T(1,128)} %param.14) | copy-start | bytes 98308
  19.9 19.0 %collective-permute-start.4 = (bf16[1,128]{1,0:T(2,128)(2,1)S(1)}, bf16[1,128]{1,0:T(2,128)(2,1)S(1)}, u32[]{:S(2)}, u32[]{:S(2)}) collective-permute-start(bf16[1,128]{1,0:T(2,128)(2,1)S(1)} %copy-done.26), channel_id=1, source_target_pairs={{0,31},{1,0},{2,1},{3,2},{4,3},{5,4},{6,5},{7,6},{8,7},{9,8},{10,9... | collective-permute-start | bytes 776 | tf_op jit(solution)/shard_map/ppermute | solution.py:311
  27.8 39.8 %collective-permute-start.5 = (bf16[1456,128]{1,0:T(8,128)(2,1)S(1)}, bf16[1456,128]{1,0:T(8,128)(2,1)}, u32[]{:S(2)}, u32[]{:S(2)}) collective-permute-start(bf16[1456,128]{1,0:T(8,128)(2,1)S(1)} %slice_bitcast_fusion), channel_id=1, source_target_pairs={{0,384},{128,0},{256,128},{384,256},{1,385},{129,1},{257,129},{385... | collective-permute-start | bytes 1118216 | tf_op jit(solution)/shard_map/ppermute | solution.py:324
  37.6 30.0 %collective-permute-start.6 = (bf16[704,128]{1,0:T(8,128)(2,1)S(1)}, bf16[704,128]{1,0:T(8,128)(2,1)}, u32[]{:S(2)}, u32[]{:S(2)}) collective-permute-start(bf16[704,128]{1,0:T(8,128)(2,1)S(1)} %broadcast_select_fusion), channel_id=1, source_target_pairs={{32,416},{64,448},{160,32},{192,64},{288,160},{320,192},{416,288},... | collective-permute-start | bytes 540680 | tf_op jit(solution)/shard_map/ppermute | solution.py:331
  38.9 11.5 %copy-start.30 = (bf16[1,128]{1,0:T(2,128)(2,1)}, bf16[1,128]{1,0:T(2,128)(2,1)S(1)}, u32[]{:S(2)}) copy-start(bf16[1,128]{1,0:T(2,128)(2,1)S(1)} %collective-permute-done.4.far_energy_ref.second_energy_ref) | copy-start | bytes 772
  38.9 28.7 %collective-permute-start.7 = (bf16[1232,128]{1,0:T(8,128)(2,1)}, bf16[1232,128]{1,0:T(8,128)(2,1)S(1)}, u32[]{:S(2)}, u32[]{:S(2)}) collective-permute-start(bf16[1232,128]{1,0:T(8,128)(2,1)} %collective-permute-done.1), channel_id=1, source_target_pairs={{96,480},{224,96},{352,224},{480,352},{97,481},{225,97},{353,225},... | collective-permute-start | bytes 946184 | tf_op jit(solution)/shard_map/ppermute | solution.py:330
  50.4 6.6 %copy-start.1 = (bf16[128,4096]{1,0:T(8,128)(2,1)}, bf16[128,4096]{1,0:T(8,128)(2,1)S(1)}, u32[]{:S(2)}) copy-start(bf16[128,4096]{1,0:T(8,128)(2,1)S(1)} %get-tuple-element.29.refs_8_.column_ref) | copy-start | bytes 3145732
  68.3 9.2 %collective-permute-start.8 = (bf16[1456,128]{1,0:T(8,128)(2,1)}, bf16[1456,128]{1,0:T(8,128)(2,1)S(1)}, u32[]{:S(2)}, u32[]{:S(2)}) collective-permute-start(bf16[1456,128]{1,0:T(8,128)(2,1)} %collective-permute-done.5), channel_id=1, source_target_pairs={{0,96},{1,97},{2,98},{3,99},{4,100},{5,101},{6,102},{7,103},{8,104... | collective-permute-start | bytes 1118216 | tf_op jit(solution)/shard_map/ppermute | solution.py:341
  69.7 6.2 %collective-permute-start.10 = (bf16[704,128]{1,0:T(8,128)(2,1)}, bf16[704,128]{1,0:T(8,128)(2,1)S(1)}, u32[]{:S(2)}, u32[]{:S(2)}) collective-permute-start(bf16[704,128]{1,0:T(8,128)(2,1)} %collective-permute-done.6), channel_id=1, source_target_pairs={{64,96},{65,97},{66,98},{67,99},{68,100},{69,101},{70,102},{71,103... | collective-permute-start | bytes 540680 | tf_op jit(solution)/shard_map/ppermute | solution.py:342
  70.3 6.2 %collective-permute-start.9 = (bf16[704,128]{1,0:T(8,128)(2,1)}, bf16[704,128]{1,0:T(8,128)(2,1)S(1)}, u32[]{:S(2)}, u32[]{:S(2)}) collective-permute-start(bf16[704,128]{1,0:T(8,128)(2,1)} %collective-permute-done.6), channel_id=1, source_target_pairs={{32,96},{33,97},{34,98},{35,99},{36,100},{37,101},{38,102},{39,103... | collective-permute-start | bytes 540680 | tf_op jit(solution)/shard_map/ppermute | solution.py:342
  71.0 4.3 %collective-permute-start.12 = (bf16[1,128]{1,0:T(2,128)(2,1)S(1)}, bf16[1,128]{1,0:T(2,128)(2,1)S(1)}, u32[]{:S(2)}, u32[]{:S(2)}) collective-permute-start(bf16[1,128]{1,0:T(2,128)(2,1)S(1)} %copy-done.26), channel_id=1, source_target_pairs={{0,480},{32,0},{64,32},{96,64},{128,96},{160,128},{192,160},{224,1... | collective-permute-start | bytes 776 | tf_op jit(solution)/shard_map/ppermute | solution.py:311
  78.2 1.2 copy-start.2
  84.2 55.2 %copy-start.3 = (bf16[128,4096]{1,0:T(8,128)(2,1)S(1)}, bf16[128,4096]{1,0:T(8,128)(2,1)}, u32[]{:S(2)}) copy-start(bf16[128,4096]{1,0:T(8,128)(2,1)} %copy-done.1) | copy-start | bytes 3145732
  87.7 51.7 %copy-start.17 = (f32[128,256]{1,0:T(8,128)S(1)}, f32[128,256]{1,0:T(8,128)}, u32[]{:S(2)}) copy-start(f32[128,256]{1,0:T(8,128)} %constant.30.clone.into_ref) | copy-start | bytes 393220
  106.9 32.5 %copy-start.20 = (f32[64,32]{1,0:T(8,128)S(1)}, f32[64,32]{1,0:T(8,128)}, u32[]{:S(2)}) copy-start(f32[64,32]{1,0:T(8,128)} %constant.29.clone.odd_ref) | copy-start | bytes 24580
  127.2 12.2 %copy-start.18 = (f32[128,128]{1,0:T(8,128)S(1)}, f32[128,128]{1,0:T(8,128)}, u32[]{:S(2)}) copy-start(f32[128,128]{1,0:T(8,128)} %constant.31.clone.back_ref) | copy-start | bytes 196612
  127.2 12.2 %copy-start.19 = (f32[64,128]{1,0:T(8,128)S(1)}, f32[64,128]{1,0:T(8,128)}, u32[]{:S(2)}) copy-start(f32[64,128]{1,0:T(8,128)} %constant.32.clone.screen_ref) | copy-start | bytes 98308
  140.0 1.2 copy-start.5
  (22 other events, 17.6 us)

commit v4 on v3

--- a/solution.py
+++ b/solution.py
@@ -24,7 +24,6 @@
 LANES = 128
 ROWS = GRID // LANES
 STEP = 512
-LIMIT = 24 * 1024 * 1024
 
 SMEAR = 0.5
 FERMI = 0.0
@@ -132,8 +131,22 @@
 UNROLL = 32
 
 
+def started(sems, *pairs, first=0):
+    copies = []
+    for index, (source, target) in enumerate(pairs):
+        copies.append(pltpu.make_async_copy(source, target, sems.at[first + index]))
+        copies[-1].start()
+    return copies
+
+
+def finished(copies):
+    for copy in copies:
+        copy.wait()
+
+
 def prepare_kernel(order_smem, own_ref, order_ref, external_ref,
-                   turned_ref, moved_ref, weighted_ref, column_ref, wide, scattered, parts, potential):
+                   turned_out, moved_out, weighted_out, column_out,
+                   turned_ref, moved_ref, weighted_ref, column_ref, wide, scattered, parts, potential, sems):
     wide[...] = own_ref[...].astype(jnp.float32)
 
     def move(step, carry):
@@ -155,12 +168,16 @@
         return carry
 
     lax.fori_loop(0, ROWS, turn, 0)
+    copies = started(sems, (turned_ref, turned_out), (moved_ref, moved_out), (column_ref, column_out))
     potential[...] = to_far_order(external_ref, order_ref, column_ref, parts)
     weigh(potential, moved_ref, weighted_ref)
-
-
-def second_kernel(order_smem, sent_ref, turned_ref, external_ref, energy_ref, far_energy_ref,
-                  far_ref, terms_ref, wide, gathered, weighted):
+    copies += started(sems, (weighted_ref, weighted_out), first=3)
+    finished(copies)
+
+
+def second_kernel(order_smem, sent_ref, turned_in, external_ref, energy_ref, far_energy_ref,
+                  far_out, terms_ref, wide, gathered, weighted, turned_ref, far_ref, sems):
+    loads = started(sems, (turned_in, turned_ref))
     wide[...] = sent_ref[...].astype(jnp.float32)
 
     def move(step, carry):
@@ -172,29 +189,38 @@
 
     lax.fori_loop(0, GRID // UNROLL, move, 0)
     far_ref[...] = gathered[...].astype(jnp.bfloat16)
+    stores = started(sems, (far_ref, far_out), first=1)
+    finished(loads)
     weigh(external_ref, turned_ref, weighted)
     respond(weighted, far_ref, turned_ref, weights(energy_ref[...], far_energy_ref[...]), terms_ref)
+    finished(stores)
 
 
 def first_kernel(flag_smem, *refs):
     piece_refs = refs[:4]
-    (beside_ref, moved_ref, weighted_ref, order_ref, column_ref, energy_ref, far_energy_ref, other_ref,
-     far_ref, terms_ref, own_terms) = refs[4:]
+    (beside_ref, moved_in, weighted_in, order_ref, column_in, energy_ref, far_energy_ref, other_ref,
+     far_out, terms_ref, own_terms, far_ref, moved_ref, weighted_ref, column_ref, sems) = refs[4:]
+    loads = started(sems, (weighted_in, weighted_ref), (moved_in, moved_ref), (column_in, column_ref))
 
     @pl.when(flag_smem[0] == 1)
     def _():
-        start = 0
+        start, pairs = 0, []
         for piece in piece_refs:
-            far_ref[start : start + piece.shape[0], :] = piece[...]
+            pairs.append((piece, far_ref.at[pl.ds(start, piece.shape[0])]))
             start += piece.shape[0]
+        finished(started(sems, *pairs, first=4))
 
     @pl.when(flag_smem[0] == 0)
     def _():
-        far_ref[...] = beside_ref[...]
-
-    respond(weighted_ref, far_ref, moved_ref, weights(energy_ref[...], far_energy_ref[...]), own_terms)
+        finished(started(sems, (beside_ref, far_ref), first=8))
+
+    stores = started(sems, (far_ref, far_out), first=3)
+    weight = weights(energy_ref[...], far_energy_ref[...])
+    finished(loads)
+    respond(weighted_ref, far_ref, moved_ref, weight, own_terms)
     from_far_order(own_terms[...], order_ref, column_ref, terms_ref, 0)
     terms_ref[ROWS:, :] = other_ref[...]
+    finished(stores)
 
 
 def exact_dot(left, right):
@@ -202,9 +228,12 @@
 
 
 def last_kernel(density_ref, external_ref, even_ref, odd_ref, into_ref, back_ref, screen_ref, even_t_ref, odd_t_ref,
-                first_ref, second_ref, moved_ref, turned_ref, order_ref, column_ref,
+                first_in, second_in, moved_in, turned_in, order_ref, column_in,
                 energy_ref, first_energy_ref, second_energy_ref,
-                response_ref, terms_ref, parts, potential, moved_potential, weighted, own_terms):
+                response_ref, terms_ref, parts, potential, moved_potential, weighted, own_terms,
+                first_ref, second_ref, moved_ref, turned_ref, column_ref, sems):
+    loads = started(sems, (column_in, column_ref), (moved_in, moved_ref), (first_in, first_ref))
+    later = started(sems, (turned_in, turned_ref), (second_in, second_ref), first=3)
     scale = 1.0 / math.sqrt(math.prod(AXIS_SIZES))
     low_half = lax.broadcasted_iota(jnp.int32, (ROWS, LANES), 1) < GY
     along_y = exact_dot(density_ref[...] * scale, into_ref[...])
@@ -214,11 +243,13 @@
         back = exact_dot(spectrum * screen_ref[...], back_ref[...])
         field = jnp.where(low_half, exact_dot(even_t_ref[...], back), exact_dot(odd_t_ref[...], back))
         potential[at, :] = external_ref[...] + field
+    finished(loads)
     moved_potential[...] = to_far_order(potential.at[0:ROWS], order_ref, column_ref, parts)
     weigh(moved_potential, moved_ref, weighted)
     weight = weights(energy_ref[...], first_energy_ref[...])
     response_ref[0] = respond(weighted, first_ref, moved_ref, weight, own_terms).T
     from_far_order(own_terms[...], order_ref, column_ref, terms_ref, 0)
+    finished(later)
     weigh(potential.at[ROWS : 2 * ROWS], turned_ref, weighted)
     weight = weights(energy_ref[...], second_energy_ref[...])
     response_ref[1] = respond(weighted, second_ref, turned_ref, weight, own_terms).T
@@ -240,17 +271,17 @@
 
 VMEM = pl.BlockSpec(memory_space=pltpu.VMEM)
 SMEM = pl.BlockSpec(memory_space=pltpu.SMEM)
-
-
-def local_call(kernel, smem, arrays, outs, scratch, microseconds):
+HBM = pl.BlockSpec(memory_space=pltpu.HBM)
+
+
+def local_call(kernel, arrays, in_specs, outs, scratch, copies, microseconds):
     return pl.pallas_call(
         kernel,
-        out_shape=[jax.ShapeDtypeStruct(shape, kind) for shape, kind in outs],
-        in_specs=[SMEM] * smem + [VMEM] * (len(arrays) - smem),
-        out_specs=[VMEM] * len(outs),
-        scratch_shapes=[pltpu.VMEM(shape, kind) for shape, kind in scratch],
+        out_shape=[jax.ShapeDtypeStruct(shape, kind) for shape, kind, spec in outs],
+        in_specs=in_specs,
+        out_specs=[spec for shape, kind, spec in outs],
+        scratch_shapes=[pltpu.VMEM(shape, kind) for shape, kind in scratch] + [pltpu.SemaphoreType.DMA((copies,))],
         cost_estimate=pl.CostEstimate(flops=0, bytes_accessed=microseconds * 3000000, transcendentals=0),
-        compiler_params=pltpu.CompilerParams(vmem_limit_bytes=LIMIT),
     )(*arrays)
 
 
@@ -263,31 +294,38 @@
 
 def prepare(order, own, order_blocks, external):
     return local_call(
-        prepare_kernel, 1, (order, own, order_blocks, external),
-        [(TURNED, BF16)] * 3 + [((LANES, GRID), BF16)],
-        [(TALL, F32), (TALL, F32), ((3 * ROWS, GRID), BF16), (BLOCKS, F32)], 12,
+        prepare_kernel, (order, own, order_blocks, external), [SMEM, VMEM, VMEM, VMEM],
+        [(TURNED, BF16, HBM)] * 4,
+        [(TURNED, BF16)] * 4 + [(TALL, F32), (TALL, F32), ((3 * ROWS, GRID), BF16), (BLOCKS, F32)], 4, 10,
     )
 
 
 def second_round_one(order, sent, turned, external, energy, far_energy):
     return local_call(
-        second_kernel, 1, (order, sent, turned, external, energy, far_energy),
-        [(TALL, BF16), (BLOCKS, F32)], [(TALL, F32), (TALL, F32), (TURNED, BF16)], 12,
+        second_kernel, (order, sent, turned, external, energy, far_energy),
+        [SMEM, VMEM, HBM, VMEM, VMEM, VMEM],
+        [(TALL, BF16, HBM), (BLOCKS, F32, VMEM)],
+        [(TALL, F32), (TALL, F32), (TURNED, BF16), (TURNED, BF16), (TALL, BF16)], 2, 7,
     )
 
 
 def first_round_one(flag, pieces, beside, moved, weighted, order_blocks, column, energy, far_energy, other):
     arrays = (flag, *pieces, beside, moved, weighted, order_blocks, column, energy, far_energy, other)
-    return local_call(first_kernel, 1, arrays, [(TALL, BF16), ((2 * ROWS, LANES), F32)], [(BLOCKS, F32)], 3)
+    return local_call(
+        first_kernel, arrays, [SMEM] + [HBM] * 5 + [HBM, HBM, VMEM, HBM, VMEM, VMEM, VMEM],
+        [(TALL, BF16, HBM), ((2 * ROWS, LANES), F32, VMEM)],
+        [(BLOCKS, F32), (TALL, BF16)] + [(TURNED, BF16)] * 3, 9, 3,
+    )
 
 
 def round_two(density, external, first, second, moved, turned, order_blocks, column, energy, first_energy, second_energy):
     arrays = (density, external, *[jnp.asarray(part) for part in coulomb_tables()], first, second, moved, turned,
               order_blocks, column, energy, first_energy, second_energy)
     return local_call(
-        last_kernel, 0, arrays,
-        [((NQ, BANDS, BANDS), F32), ((2 * ROWS, LANES), F32)],
-        [((3 * ROWS, GRID), BF16), ((2 * ROWS, LANES), F32), (BLOCKS, F32), (TURNED, BF16), (BLOCKS, F32)], 5,
+        last_kernel, arrays, [VMEM] * 9 + [HBM] * 4 + [VMEM, HBM, VMEM, VMEM, VMEM],
+        [((NQ, BANDS, BANDS), F32, VMEM), ((2 * ROWS, LANES), F32, VMEM)],
+        [((3 * ROWS, GRID), BF16), ((2 * ROWS, LANES), F32), (BLOCKS, F32), (TURNED, BF16), (BLOCKS, F32)]
+        + [(TALL, BF16)] * 2 + [(TURNED, BF16)] * 3, 5, 5,
     )
 
 
@@ -317,7 +355,7 @@
     order_blocks = reorder[0, 0].reshape(BLOCKS)
     column_index = lax.axis_index("x")
 
-    cuts = (0, 1456, 2160, 2864, GRID)
+    cuts = (0, 1360, 2064, 2768, GRID)
     parts = [orbital[cuts[c] : cuts[c + 1]] for c in range(4)]
     count = lax.axis_size("zh")
     hops = [(4 * source, 4 * ((source - 1) % count)) for source in range(count)]
@@ -333,13 +371,10 @@
     first_energy = next_along(energies, KX)
 
     turned, moved, weighted, column = prepare(reorder[0, 0], own, order_blocks, external)
-    second_states, second_terms = second_round_one(
-        reorder[1, 0], far_second, turned, external, energies, second_energy
-    )
-
-    second_terms, hop0, hop12, hop3 = lax.optimization_barrier((second_terms, hop0, hop12, hop3))
+    column, hop0, hop12, hop3 = lax.optimization_barrier((column, hop0, hop12, hop3))
     pieces = [lax.ppermute(hop0, "x", [(0, 3)])]
     pieces += [lax.ppermute(hop12, "x", [(x, 3)]) for x in (1, 2)]
+    second_states, second_terms = second_round_one(reorder[1, 0], far_second, turned, external, energies, second_energy)
     flag = (column_index == 3).astype(jnp.int32).reshape(1)
     first_states, terms = first_round_one(
         flag, pieces + [hop3], beside, moved, weighted, order_blocks, column, energies, first_energy, second_terms

time: 188 us -> 180 us (0.957)
  starting transfers between devices: 40.7 us -> 60.4 us
  local copies, waits for them, and re-layouts: 21.4 us -> 4.88 us
  waiting for transfers between devices: 11.7 us -> 1.48 us
  blocking collectives: 88.1 us -> 81.8 us
  Pallas kernels: 23 us -> 29.2 us
    ppermute x3, starting transfers between devices: 18.5 us -> 37.3 us  [next_along(): lax.ppermute(value, axis, [(source, (source - 1) % count) for source in r...]
    unnamed x66 -> x20, local copies, waits for them, and re-layouts: 19.3 us -> 1.18 us
    ppermute x1, waiting for transfers between devices: 8.98 us -> 0.01 us  [iterate(): hop0 = lax.ppermute(parts[0], KX, hops)]
    all_to_all x6, blocking collectives: 88.1 us -> 81.8 us  [exchange(): return lax.all_to_all(value, axes, 0, 0, tiled=True)]
    pallas_call x4, Pallas kernels: 23 us -> 29.2 us  [local_call(): pl.pallas_call(kernel, out_shape=[jax.ShapeDtypeStruct(shape, kind) for s...]
  transfers between devices with their start and end apart: 13 -> 13, of which waited for: 3 -> 1; matrix products, arithmetic and copies ran while one was open for 1% -> 2% of each run, Pallas kernels for 8% -> 10%
where the time goes in v4:
time: 180 us
  blocking collectives  81.8 us (45%)
  starting transfers between devices  60.4 us (34%)
  Pallas kernels  29.2 us (16%)
  local copies, waits for them, and re-layouts  4.88 us (3%)
    all_to_all x6, blocking collectives, exchange(): return lax.all_to_all(value, axes, 0, 0, tiled=True)  81.8 us
    ppermute x3, starting transfers between devices, next_along(): lax.ppermute(value, axis, [(source, (source - 1) % count) for source in r...  37.3 us
    pallas_call x4, Pallas kernels, local_call(): pl.pallas_call(kernel, out_shape=[jax.ShapeDtypeStruct(shape, kind) for s...  29.2 us
    ppermute x1, starting transfers between devices, iterate(): hop0 = lax.ppermute(parts[0], KX, hops)  10 us
    ppermute x3, starting transfers between devices, iterate(): spread = [lax.ppermute(parts[c], 'x', [(0, c)]) for c in range(1, 4)]  6.09 us
  transfers between devices with their start and end apart: 13, of which 1 were waited for; matrix products, arithmetic and copies ran while one was open for 2% of the time, Pallas kernels for 10%

profile of v4, /device:TPU:1, one launch (start us, length us, event | category | flops | bytes accessed | tf_op | source)
XLA Modules:
  0.0 179.6 jit_solution(12090978824864981544)
XLA Ops:
  0.6 8.7 %collective-permute-start.11 = (bf16[4096,128]{1,0:T(8,128)(2,1)}, bf16[4096,128]{1,0:T(8,128)(2,1)S(1)}, u32[]{:S(2)}, u32[]{:S(2)}) collective-permute-start(bf16[4096,128]{1,0:T(8,128)(2,1)} %bitcast.21), channel_id=1, source_target_pairs={{0,31},{1,0},{2,1},{3,2},{4,3},{5,4},{6,5},{7,6},{8,7},{9,8},{10,9... | collective-permute-start | bytes 3145736 | tf_op jit(solution)/shard_map/ppermute | solution.py:349
  9.4 1.3 collective-permute-start.9
  10.7 1.0 slice_bitcast_fusion.1
  11.7 2.0 %collective-permute-start = (bf16[1328,128]{1,0:T(8,128)(2,1)S(1)}, bf16[1328,128]{1,0:T(8,128)(2,1)}, u32[]{:S(2)}, u32[]{:S(2)}) collective-permute-start(bf16[1328,128]{1,0:T(8,128)(2,1)S(1)} %slice_bitcast_fusion.1), channel_id=1, source_target_pairs={{0,96},{1,97},{2,98},{3,99},{4,100},{5,101},{6,102},{7,103},{8,104... | collective-permute-start | bytes 1019912 | tf_op jit(solution)/shard_map/ppermute | solution.py:363
  13.7 1.0 slice_bitcast_fusion.2
  14.8 1.3 collective-permute-start.2
  16.1 2.7 %collective-permute-start.1 = (bf16[704,128]{1,0:T(8,128)(2,1)S(1)}, bf16[704,128]{1,0:T(8,128)(2,1)S(1)}, u32[]{:S(2)}, u32[]{:S(2)}) collective-permute-start(bf16[704,128]{1,0:T(8,128)(2,1)S(1)} %get-tuple-element.43), channel_id=1, source_target_pairs={{0,32},{1,33},{2,34},{3,35},{4,36},{5,37},{6,38},{7,39},{8,40},{9,... | collective-permute-start | bytes 540680 | tf_op jit(solution)/shard_map/ppermute | solution.py:363
  18.8 1.0 slice_bitcast_fusion
  19.9 10.0 %collective-permute-start.3 = (bf16[1360,128]{1,0:T(8,128)(2,1)S(1)}, bf16[1360,128]{1,0:T(8,128)(2,1)}, u32[]{:S(2)}, u32[]{:S(2)}) collective-permute-start(bf16[1360,128]{1,0:T(8,128)(2,1)S(1)} %slice_bitcast_fusion), channel_id=1, source_target_pairs={{0,384},{128,0},{256,128},{384,256},{1,385},{129,1},{257,129},{385... | collective-permute-start | bytes 1044488 | tf_op jit(solution)/shard_map/ppermute | solution.py:362
  30.6 0.7 collective-permute-start.5
  32.0 10.7 %shard_map.122 = (bf16[128,4096]{1,0:T(8,128)(2,1)}, bf16[128,4096]{1,0:T(8,128)(2,1)}, bf16[128,4096]{1,0:T(8,128)(2,1)}, bf16[128,4096]{1,0:T(8,128)(2,1)}) custom-call(s32[4096]{0:T(1024)} %bitcast.24, bf16[4096,128]{1,0:T(8,128)(2,1)} %bitcast.23, s32[32,128]{1,0:T(8,128)} %bitcast.25, f32[32,128]{1,0:T(8,128)} %bitcast.28), custom_call_target="tpu_custom_call" | custom-call | bytes 30000000 | tf_op jit(solution)/shard_map/pallas_call | solution.py:278
  42.8 3.0 %collective-permute-start.6 = (bf16[1360,128]{1,0:T(8,128)(2,1)}, bf16[1360,128]{1,0:T(8,128)(2,1)S(1)}, u32[]{:S(2)}, u32[]{:S(2)}) collective-permute-start(bf16[1360,128]{1,0:T(8,128)(2,1)} %collective-permute-done.3), channel_id=1, source_target_pairs={{0,96},{1,97},{2,98},{3,99},{4,100},{5,101},{6,102},{7,103},{8,104... | collective-permute-start | bytes 1044488 | tf_op jit(solution)/shard_map/ppermute | solution.py:375
  45.8 22.0 %collective-permute-start.12 = (bf16[1,128]{1,0:T(2,128)(2,1)S(1)}, bf16[1,128]{1,0:T(2,128)(2,1)S(1)}, u32[]{:S(2)}, u32[]{:S(2)}) collective-permute-start(bf16[1,128]{1,0:T(2,128)(2,1)S(1)} %copy-done.7), channel_id=1, source_target_pairs={{0,31},{1,0},{2,1},{3,2},{4,3},{5,4},{6,5},{7,6},{8,7},{9,8},{10,9... | collective-permute-start | bytes 776 | tf_op jit(solution)/shard_map/ppermute | solution.py:349
  68.5 1.4 collective-permute-done.12.far_energy_ref.second_energy_ref
  70.7 6.5 %collective-permute-start.10 = (bf16[1,128]{1,0:T(2,128)(2,1)S(1)}, bf16[1,128]{1,0:T(2,128)(2,1)S(1)}, u32[]{:S(2)}, u32[]{:S(2)}) collective-permute-start(bf16[1,128]{1,0:T(2,128)(2,1)S(1)} %copy-done.7), channel_id=1, source_target_pairs={{0,480},{32,0},{64,32},{96,64},{128,96},{160,128},{192,160},{224,1... | collective-permute-start | bytes 776 | tf_op jit(solution)/shard_map/ppermute | solution.py:349
  77.2 7.0 %shard_map.123 = (bf16[4096,128]{1,0:T(8,128)(2,1)}, f32[32,128]{1,0:T(8,128)}) custom-call(s32[4096]{0:T(1024)} %bitcast.32, bf16[4096,128]{1,0:T(8,128)(2,1)} %copy-done, bf16[128,4096]{1,0:T(8,128)(2,1)} %get-tuple-element.29.turned_in, f32[32,128]{1,0:T(8,128)} %bitcast.29, bf16[1,128]{1,0:T(2,128)(2,1)} %energy_ref.3, bf16[1,128]{1,0:T(2,128)(2,1)} %copy-done.9), custom_call_target="tpu_custom_call" | custom-call | bytes 21000000 | tf_op jit(solution)/shard_map/pallas_call | solution.py:278
  85.4 4.9 %shard_map.124 = (bf16[4096,128]{1,0:T(8,128)(2,1)}, f32[64,128]{1,0:T(8,128)}) custom-call(s32[1]{0:T(128)} %bitcast.flag_smem, bf16[1360,128]{1,0:T(8,128)(2,1)} %copy-done.2, bf16[704,128]{1,0:T(8,128)(2,1)} %copy-done.5, bf16[704,128]{1,0:T(8,128)(2,1)} %copy-done.4, bf16[1328,128]{1,0:T(8,128)(2,1)} %copy-done.3, bf16[4096,128]{1,0:T(8,128)(2,1)} %copy-done.1, ...), custom_call_target="tpu_custom_call" | custom-call | bytes 9000000 | tf_op jit(solution)/shard_map/pallas_call | solution.py:278
  90.3 13.6 %all_to_all.30 = f32[32,2,128]{2,1,0:T(2,128)S(1)} all-to-all(f32[32,2,128]{2,1,0:T(2,128)} %bitcast.34), channel_id=1, replica_groups=mesh['zh'=4,'x'=4,'y'=4,'zl'=4,'core'=2] {'x','y','core'}, dimensions={0} | all-to-all | bytes 65536 | tf_op jit(solution)/shard_map/all_to_all | solution.py:333
  104.0 18.7 %all_to_all.31 = f32[16,2,128]{2,1,0:T(2,128)S(1)} all-to-all(f32[16,2,128]{2,1,0:T(2,128)S(1)} %broadcast_in_dim.8), channel_id=1, replica_groups=mesh['zh'=4,'x'=4,'y'=4,'zl'=4,'core'=2] {'zh','zl'}, dimensions={0} | all-to-all | bytes 32768 | tf_op jit(solution)/shard_map/all_to_all | solution.py:333
  122.7 12.4 %all_to_all.32 = f32[32,2,128]{2,1,0:T(2,128)} all-to-all(f32[32,2,128]{2,1,0:T(2,128)S(1)} %broadcast_in_dim.9), channel_id=1, replica_groups=mesh['zh'=4,'x'=4,'y'=4,'zl'=4,'core'=2] {'x','y','core'}, dimensions={0} | all-to-all | bytes 65536 | tf_op jit(solution)/shard_map/all_to_all | solution.py:333
  135.2 6.6 %shard_map.125 = (f32[2,128,128]{2,1,0:T(8,128)}, f32[64,128]{1,0:T(8,128)}) custom-call(f32[64,128]{1,0:T(8,128)} %bitcast.31, f32[32,128]{1,0:T(8,128)} %bitcast.30, f32[64,32]{1,0:T(8,128)} %constant.28.clone.even_ref, f32[64,32]{1,0:T(8,128)} %constant.29.clone.odd_ref, f32[128,256]{1,0:T(8,128)} %constant.30.clone.into_ref, ...), custom_call_target="tpu_custom_call" | custom-call | bytes 15000000 | tf_op jit(solution)/shard_map/pallas_call | solution.py:278
  141.8 11.3 %all_to_all.33 = f32[32,2,128]{2,1,0:T(2,128)S(1)} all-to-all(f32[32,2,128]{2,1,0:T(2,128)} %bitcast.33), channel_id=1, replica_groups=mesh['zh'=4,'x'=4,'y'=4,'zl'=4,'core'=2] {'x','y','core'}, dimensions={0} | all-to-all | bytes 65536 | tf_op jit(solution)/shard_map/all_to_all | solution.py:333
  153.1 13.9 %all_to_all.34 = f32[16,2,128]{2,1,0:T(2,128)S(1)} all-to-all(f32[16,2,128]{2,1,0:T(2,128)S(1)} %broadcast_in_dim.10), channel_id=1, replica_groups=mesh['zh'=4,'x'=4,'y'=4,'zl'=4,'core'=2] {'zh','zl'}, dimensions={0} | all-to-all | bytes 32768 | tf_op jit(solution)/shard_map/all_to_all | solution.py:333
  167.0 11.9 %all_to_all.35 = f32[32,2,128]{2,1,0:T(2,128)S(1)} all-to-all(f32[32,2,128]{2,1,0:T(2,128)S(1)} %broadcast_in_dim.11), channel_id=1, replica_groups=mesh['zh'=4,'x'=4,'y'=4,'zl'=4,'core'=2] {'x','y','core'}, dimensions={0} | all-to-all | bytes 65536 | tf_op jit(solution)/shard_map/all_to_all | solution.py:333
  (46 shorter events, 4.7 us)
Async XLA Ops:
  0.6 70.0 %collective-permute-start.11 = (bf16[4096,128]{1,0:T(8,128)(2,1)}, bf16[4096,128]{1,0:T(8,128)(2,1)S(1)}, u32[]{:S(2)}, u32[]{:S(2)}) collective-permute-start(bf16[4096,128]{1,0:T(8,128)(2,1)} %bitcast.21), channel_id=1, source_target_pairs={{0,31},{1,0},{2,1},{3,2},{4,3},{5,4},{6,5},{7,6},{8,7},{9,8},{10,9... | collective-permute-start | bytes 3145736 | tf_op jit(solution)/shard_map/ppermute | solution.py:349
  9.4 74.9 %collective-permute-start.9 = (bf16[4096,128]{1,0:T(8,128)(2,1)}, bf16[4096,128]{1,0:T(8,128)(2,1)S(1)}, u32[]{:S(2)}, u32[]{:S(2)}) collective-permute-start(bf16[4096,128]{1,0:T(8,128)(2,1)} %bitcast.22), channel_id=1, source_target_pairs={{32,0},{64,32},{96,64},{33,1},{65,33},{97,65},{34,2},{66,34},{98,6... | collective-permute-start | bytes 3145736 | tf_op jit(solution)/shard_map/ppermute | solution.py:365
  11.7 18.3 %collective-permute-start = (bf16[1328,128]{1,0:T(8,128)(2,1)S(1)}, bf16[1328,128]{1,0:T(8,128)(2,1)}, u32[]{:S(2)}, u32[]{:S(2)}) collective-permute-start(bf16[1328,128]{1,0:T(8,128)(2,1)S(1)} %slice_bitcast_fusion.1), channel_id=1, source_target_pairs={{0,96},{1,97},{2,98},{3,99},{4,100},{5,101},{6,102},{7,103},{8,104... | collective-permute-start | bytes 1019912 | tf_op jit(solution)/shard_map/ppermute | solution.py:363
  14.8 5.1 %collective-permute-start.2 = (bf16[704,128]{1,0:T(8,128)(2,1)S(1)}, bf16[704,128]{1,0:T(8,128)(2,1)S(1)}, u32[]{:S(2)}, u32[]{:S(2)}) collective-permute-start(bf16[704,128]{1,0:T(8,128)(2,1)S(1)} %get-tuple-element.42), channel_id=1, source_target_pairs={{0,64},{1,65},{2,66},{3,67},{4,68},{5,69},{6,70},{7,71},{8,72},{9,... | collective-permute-start | bytes 540680 | tf_op jit(solution)/shard_map/ppermute | solution.py:363
  16.1 13.8 %collective-permute-start.1 = (bf16[704,128]{1,0:T(8,128)(2,1)S(1)}, bf16[704,128]{1,0:T(8,128)(2,1)S(1)}, u32[]{:S(2)}, u32[]{:S(2)}) collective-permute-start(bf16[704,128]{1,0:T(8,128)(2,1)S(1)} %get-tuple-element.43), channel_id=1, source_target_pairs={{0,32},{1,33},{2,34},{3,35},{4,36},{5,37},{6,38},{7,39},{8,40},{9,... | collective-permute-start | bytes 540680 | tf_op jit(solution)/shard_map/ppermute | solution.py:363
  19.8 11.5 %copy-start.6 = (s32[2,1,4096]{2,1,0:T(1,128)S(1)}, s32[2,1,4096]{2,1,0:T(1,128)}, u32[]{:S(2)}) copy-start(s32[2,1,4096]{2,1,0:T(1,128)} %param.14) | copy-start | bytes 98308
  19.9 22.8 %collective-permute-start.3 = (bf16[1360,128]{1,0:T(8,128)(2,1)S(1)}, bf16[1360,128]{1,0:T(8,128)(2,1)}, u32[]{:S(2)}, u32[]{:S(2)}) collective-permute-start(bf16[1360,128]{1,0:T(8,128)(2,1)S(1)} %slice_bitcast_fusion), channel_id=1, source_target_pairs={{0,384},{128,0},{256,128},{384,256},{1,385},{129,1},{257,129},{385... | collective-permute-start | bytes 1044488 | tf_op jit(solution)/shard_map/ppermute | solution.py:362
  30.0 12.8 %collective-permute-start.4 = (bf16[704,128]{1,0:T(8,128)(2,1)S(1)}, bf16[704,128]{1,0:T(8,128)(2,1)S(1)}, u32[]{:S(2)}, u32[]{:S(2)}) collective-permute-start(bf16[704,128]{1,0:T(8,128)(2,1)S(1)} %broadcast_select_fusion), channel_id=1, source_target_pairs={{32,416},{64,448},{160,32},{192,64},{288,160},{320,192},{416,288},... | collective-permute-start | bytes 540680 | tf_op jit(solution)/shard_map/ppermute | solution.py:369
  30.6 12.1 %collective-permute-start.5 = (bf16[1328,128]{1,0:T(8,128)(2,1)}, bf16[1328,128]{1,0:T(8,128)(2,1)S(1)}, u32[]{:S(2)}, u32[]{:S(2)}) collective-permute-start(bf16[1328,128]{1,0:T(8,128)(2,1)} %collective-permute-done), channel_id=1, source_target_pairs={{96,480},{224,96},{352,224},{480,352},{97,481},{225,97},{353,225},... | collective-permute-start | bytes 1019912 | tf_op jit(solution)/shard_map/ppermute | solution.py:368
  42.7 3.1 %copy-start.7 = (bf16[1,128]{1,0:T(2,128)(2,1)S(1)}, bf16[1,128]{1,0:T(2,128)(2,1)}, u32[]{:S(2)}) copy-start(bf16[1,128]{1,0:T(2,128)(2,1)} %energy_ref.3) | copy-start | bytes 772
  42.7 41.4 %copy-start.3 = (bf16[1328,128]{1,0:T(8,128)(2,1)}, bf16[1328,128]{1,0:T(8,128)(2,1)S(1)}, u32[]{:S(2)}) copy-start(bf16[1328,128]{1,0:T(8,128)(2,1)S(1)} %collective-permute-done.5.refs_3_) | copy-start | bytes 1019908
  42.8 41.5 %collective-permute-start.6 = (bf16[1360,128]{1,0:T(8,128)(2,1)}, bf16[1360,128]{1,0:T(8,128)(2,1)S(1)}, u32[]{:S(2)}, u32[]{:S(2)}) collective-permute-start(bf16[1360,128]{1,0:T(8,128)(2,1)} %collective-permute-done.3), channel_id=1, source_target_pairs={{0,96},{1,97},{2,98},{3,99},{4,100},{5,101},{6,102},{7,103},{8,104... | collective-permute-start | bytes 1044488 | tf_op jit(solution)/shard_map/ppermute | solution.py:375
  45.8 24.1 %collective-permute-start.12 = (bf16[1,128]{1,0:T(2,128)(2,1)S(1)}, bf16[1,128]{1,0:T(2,128)(2,1)S(1)}, u32[]{:S(2)}, u32[]{:S(2)}) collective-permute-start(bf16[1,128]{1,0:T(2,128)(2,1)S(1)} %copy-done.7), channel_id=1, source_target_pairs={{0,31},{1,0},{2,1},{3,2},{4,3},{5,4},{6,5},{7,6},{8,7},{9,8},{10,9... | collective-permute-start | bytes 776 | tf_op jit(solution)/shard_map/ppermute | solution.py:349
  67.8 16.4 %collective-permute-start.8 = (bf16[704,128]{1,0:T(8,128)(2,1)S(1)}, bf16[704,128]{1,0:T(8,128)(2,1)S(1)}, u32[]{:S(2)}, u32[]{:S(2)}) collective-permute-start(bf16[704,128]{1,0:T(8,128)(2,1)S(1)} %collective-permute-done.4), channel_id=1, source_target_pairs={{64,96},{65,97},{66,98},{67,99},{68,100},{69,101},{70,102},{71,103... | collective-permute-start | bytes 540680 | tf_op jit(solution)/shard_map/ppermute | solution.py:376
  70.0 0.7 copy-start.9
  70.0 14.3 %collective-permute-start.7 = (bf16[704,128]{1,0:T(8,128)(2,1)S(1)}, bf16[704,128]{1,0:T(8,128)(2,1)S(1)}, u32[]{:S(2)}, u32[]{:S(2)}) collective-permute-start(bf16[704,128]{1,0:T(8,128)(2,1)S(1)} %collective-permute-done.4), channel_id=1, source_target_pairs={{32,96},{33,97},{34,98},{35,99},{36,100},{37,101},{38,102},{39,103... | collective-permute-start | bytes 540680 | tf_op jit(solution)/shard_map/ppermute | solution.py:376
  70.7 6.5 %copy-start = (bf16[4096,128]{1,0:T(8,128)(2,1)}, bf16[4096,128]{1,0:T(8,128)(2,1)S(1)}, u32[]{:S(2)}) copy-start(bf16[4096,128]{1,0:T(8,128)(2,1)S(1)} %collective-permute-done.11.sent_ref) | copy-start | bytes 3145732
  70.7 13.5 %collective-permute-start.10 = (bf16[1,128]{1,0:T(2,128)(2,1)S(1)}, bf16[1,128]{1,0:T(2,128)(2,1)S(1)}, u32[]{:S(2)}, u32[]{:S(2)}) collective-permute-start(bf16[1,128]{1,0:T(2,128)(2,1)S(1)} %copy-done.7), channel_id=1, source_target_pairs={{0,480},{32,0},{64,32},{96,64},{128,96},{160,128},{192,160},{224,1... | collective-permute-start | bytes 776 | tf_op jit(solution)/shard_map/ppermute | solution.py:349
  84.2 0.6 copy-start.8
  84.2 0.7 copy-start.4
  84.2 0.8 copy-start.5
  84.3 0.8 copy-start.2
  84.3 1.2 copy-start.1
